TPU v7x, 32 devices: a whole 2x2x4 slice. The times are simulated.
32 devices in a mesh: coil: 4 (over y, x), slab: 8 (over z, core).
Axes of the slice: x: 2, y: 2, z: 4, core: 2. Of those that a mesh axis runs over, the one named last changes fastest.
Arguments:
- coil_maps: float32 [8, 2, 8, 256, 128], P('coil', None, 'slab'), may hold values from -1.5 to 1.5
- kspace: float32 [8, 2, 8, 256, 128], P('coil', None, 'slab'), may hold values from -6 to 6
- sample_mask: int32 [256, 128], replicated, may hold values 0 or 1
- iterate: float32 [2, 8, 256, 128], P(None, 'slab', 'coil'), may hold values from -6 to 6
- probe_bits: int32 [2, 8, 256, 128], P(None, 'slab', 'coil'), may hold values from 0 to 1
- loss_gradient: float32 [2, 8, 256, 128], P(None, 'slab', 'coil'), may hold values from -6 to 6
- adjoint: float32 [2, 8, 256, 128], P(None, 'slab', 'coil'), may hold values from -6 to 6
- kernel_first: bfloat16 [24, 2, 3, 3, 3], replicated, may hold values from -0.875 to 0.875
- kernel_second: bfloat16 [24, 24, 3, 3, 3], replicated, may hold values from -0.25 to 0.25
- kernel_last: bfloat16 [2, 24, 3, 3, 3], replicated, may hold values from -0.25 to 0.25
Outputs:
- new_iterate: float32 [2, 8, 256, 128], P(None, 'slab', 'coil')
- probe_pullback: float32 [2, 8, 256, 128], P(None, 'slab', 'coil')
- adjoint_next: float32 [2, 8, 256, 128], P(None, 'slab', 'coil')
Inputs may be any that keep to these rules, and one draw needn't show every extreme that they name: `sample_mask`: 1 marks a sampled phase-encode line. `probe_bits`: the probe's sign is 2 p - 1.
All inputs are finite; a program needn't handle non-finite values.
Results may differ from a plain program's by a relative error of at most 0.0055.
Values may be sent and summed in bfloat16 or wider, within the bound.
A program may use at most 128 MiB of HBM per device.

v0:
```python
import math

import jax
import jax.numpy as jnp
import numpy as np
from jax import lax
from jax.experimental import pallas as pl
from jax.experimental.pallas import tpu as pltpu
from jax.sharding import PartitionSpec as P

step_size = 0.8
reach = 4
both = ("coil", "slab")
f32 = jnp.float32
bf16 = jnp.bfloat16
vmem = pl.BlockSpec(memory_space=pltpu.VMEM)
MESH = pl.DeviceIdType.MESH


class Channel:
    def __init__(self, axes, how, source, target, send_sem, recv_sem):
        self.axes, self.how, self.source, self.target = axes, how, source, target
        self.send_sem, self.recv_sem = send_sem, recv_sem
        self.size = math.prod(lax.axis_size(axis) for axis in axes)
        self.mine = rank_of(axes)

    def row(self, rank):
        if self.how == "all":
            return self.source
        if self.how == "slab":
            return self.source.at[place_of(self.axes, rank)[1]]
        return self.source.at[rank]

    def copy(self, source_rank, target_row, device_rank, step):
        return pltpu.make_async_remote_copy(
            src_ref=self.row(source_rank),
            dst_ref=self.target.at[target_row],
            send_sem=self.send_sem.at[step],
            recv_sem=self.recv_sem.at[step],
            device_id=place_of(self.axes, device_rank),
            device_id_type=MESH,
        )

    def start(self):
        def send(step, carry):
            rank = lax.rem(self.mine + step, self.size)
            self.copy(rank, self.mine, rank, step).start()
            return carry

        lax.fori_loop(1, self.size, send, 0)
        self.target[self.mine] = self.row(self.mine)[...]

    def finish(self):
        def wait(step, carry):
            rank = lax.rem(self.mine + self.size - step, self.size)
            self.copy(self.mine, rank, rank, step).wait()
            return carry

        lax.fori_loop(1, self.size, wait, 0)


def rank_of(axes):
    if axes == both:
        return lax.axis_index("coil") * lax.axis_size("slab") + lax.axis_index("slab")
    return lax.axis_index(axes[0])


def place_of(axes, rank):
    slabs = lax.axis_size("slab")
    if axes == both:
        return lax.div(rank, slabs), lax.rem(rank, slabs)
    return (rank, lax.axis_index("slab")) if axes == ("coil",) else (lax.axis_index("coil"), rank)


def greet_all():
    barrier = pltpu.get_barrier_semaphore()
    size = lax.axis_size("coil") * lax.axis_size("slab")

    def greet(step, carry):
        rank = lax.rem(rank_of(both) + step, size)
        pl.semaphore_signal(barrier, inc=1, device_id=place_of(both, rank), device_id_type=MESH)
        return carry

    lax.fori_loop(1, size, greet, 0)
    return barrier, size - 1


def split(table):
    high = jnp.asarray(table, f32).astype(bf16)
    return high, (jnp.asarray(table, f32) - high.astype(f32)).astype(bf16)


def fourier_tables(height, depth, sign):
    def parts(length):
        counter = np.arange(length)
        angles = (counter[:, None] * counter[None, :] % length) * (2.0 * np.pi / length)
        return np.cos(angles) / np.sqrt(length), sign * np.sin(angles) / np.sqrt(length)

    depth_cos, depth_sin = parts(depth)
    height_cos, height_sin = parts(height)
    along = np.block([[depth_cos, depth_sin], [-depth_sin, depth_cos]])
    down = np.concatenate([height_cos, height_sin], axis=0)
    return split(along) + split(down)


def dot(left, right):
    return jnp.dot(left, right, preferred_element_type=f32)


def halves(values):
    high = values.astype(bf16)
    return high, (values - high.astype(f32)).astype(bf16)


def spectrum(values, tables):
    along_high, along_low, down_high, down_low = tables
    height, depth = values.shape[0], values.shape[1] // 2
    high, low = halves(values)
    high, low = halves(
        dot(high, along_high[...]) + (dot(low, along_high[...]) + dot(high, along_low[...]))
    )
    both_parts = dot(down_high[...], high) + (dot(down_high[...], low) + dot(down_low[...], high))
    upper, lower = both_parts[:height], both_parts[height:]
    return jnp.concatenate(
        [upper[:, :depth] - lower[:, depth:], lower[:, :depth] + upper[:, depth:]], axis=1
    )


def coil_term(real, imag, coil, maps, kspace, mask, tables):
    depth = real.shape[1]
    map_real, map_imag = maps[coil, 0, 0], maps[coil, 1, 0]
    image = jnp.concatenate(
        [map_real * real - map_imag * imag, map_real * imag + map_imag * real], axis=1
    )
    freq = spectrum(image, tables[:4])
    if kspace is not None:
        freq = freq - jnp.concatenate([kspace[coil, 0, 0], kspace[coil, 1, 0]], axis=1)
    back = spectrum(mask * freq, tables[4:])
    back_real, back_imag = back[:, :depth], back[:, depth:]
    return (
        map_real * back_real + map_imag * back_imag,
        map_real * back_imag - map_imag * back_real,
    )


def column(gathered, channel):
    return jnp.concatenate(
        [gathered[block, channel].astype(f32) for block in range(gathered.shape[0])], axis=0
    )


forms = {"in": ((2, 0, 3, 4, 1), 1, 9), "mid": ((3, 2, 0, 4, 1), 3, 3), "out": ((3, 4, 2, 0, 1), 9, 1)}


def small_kernel(kernel, form):
    order, taps, units = forms[form]
    outs, ins = kernel.shape[:2]
    return jnp.transpose(kernel, order).reshape(taps * 3 * outs, units * ins)


def band_constants(kernel, slices, form):
    _, taps, units = forms[form]
    outs, ins = kernel.shape[:2]
    spread = jnp.asarray(np.kron(np.eye(units), np.tile(np.eye(ins), (1, slices))), bf16)
    lanes = np.tile(np.repeat(np.arange(slices), ins), units)
    if form != "out":
        return spread, jnp.asarray(lanes[None, :], f32)
    row_slices = np.repeat(np.arange(slices), outs)
    bands = np.stack([lanes[None, :] == row_slices[:, None] + dx - 1 for dx in range(3)])
    repeat = np.stack(
        [
            np.kron(np.eye(taps), np.tile(np.eye(3 * outs)[dx * outs : (dx + 1) * outs], (slices, 1)))
            for dx in range(3)
        ]
    )
    return spread, jnp.asarray(bands, f32), jnp.asarray(repeat, bf16)


def build_rows(small, spread, lanes, target):
    taps, inner = target.shape[:2]
    outs = small.shape[0] // (3 * taps)
    wide = dot(small[...], spread[...])
    lane_slice = lanes[...]
    for tap in range(taps):
        blocks = []
        for out_slice in range(inner // outs):
            block = None
            for dx in range(3):
                at = (tap * 3 + dx) * outs
                term = jnp.where(lane_slice == float(out_slice + dx - 1), wide[at : at + outs], 0.0)
                block = term if block is None else block + term
            blocks.append(block)
        target[tap] = jnp.concatenate(blocks, axis=0).astype(bf16)


def build_taps(small, spread, bands, repeat, target):
    wide = dot(small[...], spread[...]).astype(bf16)
    total = None
    for dx in range(3):
        term = dot(repeat[dx], wide).reshape(target.shape) * bands[dx][None]
        total = term if total is None else total + term
    target[...] = total.astype(bf16)


def transposed(kernel):
    return jnp.swapaxes(jnp.flip(kernel, (2, 3, 4)), 0, 1)


def shifted(values, tap, depth):
    if tap == 1:
        return values
    lane = lax.broadcasted_iota(jnp.int32, (values.shape[0], depth), 1)
    edge, turn = (0, 1) if tap == 0 else (depth - 1, depth - 1)
    pieces = []
    for start in range(0, values.shape[1], depth):
        turned = pltpu.roll(values[:, start : start + depth], turn, 1)
        pieces.append(jnp.where(lane == edge, 0.0, turned))
    return jnp.concatenate(pieces, axis=1)


def conv_in(values, weights, depth):
    width = values.shape[1] - 2 * depth
    turned = [shifted(values, tap, depth) for tap in range(3)]
    stacked = jnp.concatenate(
        [turned[dz][:, dy * depth : dy * depth + width] for dy in range(3) for dz in range(3)],
        axis=0,
    )
    return dot(weights[0], stacked.astype(bf16))


def conv_mid(values, weights, depth):
    width = values.shape[1] - 2 * depth
    stacked = jnp.concatenate(
        [shifted(values, tap, depth).astype(bf16) for tap in range(3)], axis=0
    )
    total = None
    for dy in range(3):
        term = dot(weights[dy], stacked[:, dy * depth : dy * depth + width])
        total = term if total is None else total + term
    return total


def conv_out(values, weights, depth):
    width = values.shape[1] - 2 * depth
    taps, rows, inner = weights.shape
    products = dot(weights[...].reshape(taps * rows, inner), values.astype(bf16))
    total = None
    for dz in range(3):
        summed = None
        for dy in range(3):
            at = (dy * 3 + dz) * rows
            term = products[at : at + rows, dy * depth : dy * depth + width]
            summed = term if summed is None else summed + term
        term = shifted(summed, dz, depth)
        total = term if total is None else total + term
    return total


def step_kernel(maps, kspace, mask, iterate, probe_bits, adjoint, *rest):
    tables, smalls, bands, rest = rest[:8], rest[8:14], rest[14:21], rest[21:]
    in_band, mid_band, out_band = bands[:2], bands[2:4], bands[4:]
    changes = rest[0]
    (padded, work, rows_work, own_iterate, own_fields, all_iterate, all_fields, parts_send, parts,
     fields_send, fields, delta_send, delta, pulled_send, pulled, sums_send, sums, *weights) = rest[1:24]
    first, second, last, first_t, second_t, last_t = weights
    sems = rest[24:]
    channels = []
    for index, (axes, how, source, target) in enumerate((
        (("coil",), "all", own_iterate, all_iterate),
        (("coil",), "all", own_fields, all_fields),
        (("slab",), "row", fields_send, fields),
        (both, "row", parts_send, parts),
        (("slab",), "row", delta_send, delta),
        (both, "slab", pulled_send.at[0], pulled.at[0]),
        (both, "slab", pulled_send.at[1], pulled.at[1]),
        (("coil",), "row", sums_send.at[0], sums.at[0]),
        (("coil",), "row", sums_send.at[1], sums.at[1]),
    )):
        channels.append(Channel(axes, how, source, target, sems[2 * index], sems[2 * index + 1]))
    (iterate_way, field_way, window_way, part_way, delta_way, *later) = channels
    pulled_ways, sum_ways = later[:2], later[2:]

    height, depth = mask.shape
    coils, rows = all_iterate.shape[0], all_iterate.shape[2]
    pieces, _, window, _ = parts.shape
    slices = fields.shape[0]
    own = window - 2 * reach
    my_coil = lax.axis_index("coil")
    row_base = rank_of(both) * own - reach

    barrier, arrivals = greet_all()
    sign = (2 * probe_bits[...] - 1).astype(f32)
    own_iterate[...] = iterate[:, 0].astype(bf16)
    own_fields[0:2] = sign[:, 0].astype(bf16)
    own_fields[2:4] = adjoint[:, 0].astype(bf16)
    edge = jnp.zeros((6, 8, depth), f32)
    padded[:, 0:8] = edge
    padded[:, height + reach : height + reach + 8] = edge
    weight = mask[...].astype(f32)
    weight = jnp.concatenate([weight, weight], axis=1)
    pl.semaphore_wait(barrier, arrivals)
    iterate_way.start()
    field_way.start()
    iterate_way.finish()

    real, imag = column(all_iterate, 0), column(all_iterate, 1)
    total_real, total_imag = coil_term(real, imag, 0, maps, kspace, weight, tables)
    field_way.finish()
    padded[0, reach : reach + height] = real
    padded[1, reach : reach + height] = imag
    for channel in range(4):
        padded[2 + channel, reach : reach + height] = column(all_fields, channel)
    for piece in range(slices):
        start = my_coil * (slices * own) + piece * own
        fields_send[piece] = padded[:, pl.ds(start, window), :].astype(bf16)
    window_way.start()
    for coil in range(1, maps.shape[0]):
        more_real, more_imag = coil_term(real, imag, coil, maps, kspace, weight, tables)
        total_real, total_imag = total_real + more_real, total_imag + more_imag
    padded[0, reach : reach + height] = total_real
    padded[1, reach : reach + height] = total_imag
    for piece in range(pieces):
        parts_send[piece] = padded[0:2, piece * own : piece * own + window, :].astype(bf16)
    part_way.start()

    def load(values):
        work[...] = values.reshape(work.shape)
        return jnp.concatenate([work[:, row, :] for row in range(window)], axis=1)

    def cut(values, before, after):
        return values[:, before * depth : values.shape[1] - after * depth]

    def inside(values, offset):
        blocks = []
        for row in range(values.shape[1] // depth):
            at = row_base + offset + row
            keep = jnp.where((at >= 0) & (at < height), 1.0, 0.0).astype(f32)
            blocks.append(values[:, row * depth : (row + 1) * depth] * keep)
        return jnp.concatenate(blocks, axis=1)

    def store(values):
        for row in range(own):
            rows_work[:, row, :] = values[:, row * depth : (row + 1) * depth]
        return rows_work[...].reshape(slices, 2, own, depth)

    build_rows(smalls[5], *in_band, last_t)
    build_rows(smalls[0], *in_band, first)
    build_rows(smalls[1], *mid_band, second)
    build_rows(smalls[4], *mid_band, second_t)
    build_taps(smalls[2], *out_band, last)
    build_taps(smalls[3], *out_band, first_t)
    window_way.finish()
    started = load(fields[:, 0:2].astype(f32))
    grads = []
    for field in range(2):
        probe = cut(load(fields[:, 2 + 2 * field : 4 + 2 * field].astype(f32)), 1, 1)
        grads.append(conv_in(probe, last_t, depth))
    part_way.finish()
    summed = parts[0:slices].astype(f32)
    for coil in range(1, coils):
        summed = summed + parts[coil * slices : (coil + 1) * slices].astype(f32)
    moved = load(-step_size * summed)
    relaxed = started + moved
    pre1 = conv_in(relaxed.astype(bf16).astype(f32), first, depth)
    sig1 = jax.nn.sigmoid(pre1)
    act1 = inside(pre1 * sig1, 1)
    slope1 = inside(cut(sig1 * (1.0 + pre1 * (1.0 - sig1)), 2, 2), 3)
    pre2 = conv_mid(act1, second, depth)
    sig2 = jax.nn.sigmoid(pre2)
    slope2 = inside(sig2 * (1.0 + pre2 * (1.0 - sig2)), 2)
    for field in range(2):
        grad1 = conv_mid(grads[field] * slope2, second_t, depth) * slope1
        pulled_send[field] = store(conv_out(grad1, first_t, depth)).astype(bf16)
        pulled_ways[field].start()
    act2 = inside(cut(pre2 * sig2, 1, 1), 3)
    delta_send[...] = store(conv_out(act2, last, depth) + cut(moved, reach, reach))
    delta_way.start()

    for field in range(2):
        pulled_ways[field].finish()
        real = column(all_fields, 2 * field) + column(pulled.at[field], 0)
        imag = column(all_fields, 2 * field + 1) + column(pulled.at[field], 1)
        total = None
        for coil in range(maps.shape[0]):
            term = coil_term(real, imag, coil, maps, None, weight, tables)
            total = term if total is None else (total[0] + term[0], total[1] + term[1])
        for part in range(2):
            for block in range(coils):
                at = block * rows
                sums_send[field, block, part] = total[part][at : at + rows].astype(bf16)
        sum_ways[field].start()

    delta_way.finish()
    for part in range(2):
        for piece in range(slices):
            at = piece * own
            changes[0, part, at : at + own] = delta[piece, part]
    for field in range(2):
        sum_ways[field].finish()
        for part in range(2):
            added = sums[field, 0, part].astype(f32)
            for block in range(1, coils):
                added = added + sums[field, block, part].astype(f32)
            mine = jnp.concatenate(
                [
                    pulled[field, my_coil * slices + piece, part].astype(f32)
                    for piece in range(slices)
                ],
                axis=0,
            )
            changes[1 + field, part] = mine - step_size * added


def on_device(coil_maps, kspace, sample_mask, iterate, probe_bits, loss_gradient, adjoint,
              kernel_first, kernel_second, kernel_last):
    height, depth = sample_mask.shape
    coils, slabs = lax.axis_size("coil"), lax.axis_size("slab")
    pieces = coils * slabs
    own = height // pieces
    window = own + 2 * reach
    rows = iterate.shape[2]
    tables = fourier_tables(height, depth, -1.0) + fourier_tables(height, depth, 1.0)
    kernels = (kernel_first, kernel_second, kernel_last)
    smalls = [small_kernel(kernel, form) for kernel, form in zip(kernels, ("in", "mid", "out"))]
    smalls += [
        small_kernel(transposed(kernel), form) for kernel, form in zip(kernels, ("out", "mid", "in"))
    ]
    constants = [
        constant
        for kernel, form in zip(kernels, ("in", "mid", "out"))
        for constant in band_constants(kernel, slabs, form)
    ]
    hidden, channels = kernel_second.shape[0] * slabs, kernel_first.shape[1] * slabs
    buffers = [
        ((6, height + 2 * reach + 8, depth), f32),
        ((2 * slabs, window, depth), f32),
        ((2 * slabs, own, depth), f32),
        ((2, rows, depth), bf16),
        ((4, rows, depth), bf16),
        ((coils, 2, rows, depth), bf16),
        ((coils, 4, rows, depth), bf16),
        ((pieces, 2, window, depth), bf16),
        ((pieces, 2, window, depth), bf16),
        ((slabs, 6, window, depth), bf16),
        ((slabs, 6, window, depth), bf16),
        ((slabs, 2, own, depth), f32),
        ((slabs, 2, own, depth), f32),
        ((2, slabs, 2, own, depth), bf16),
        ((2, pieces, 2, own, depth), bf16),
        ((2, coils, 2, rows, depth), bf16),
        ((2, coils, 2, rows, depth), bf16),
        ((1, hidden, 9 * channels), bf16),
        ((3, hidden, 3 * hidden), bf16),
        ((9, channels, hidden), bf16),
        ((9, channels, hidden), bf16),
        ((3, hidden, 3 * hidden), bf16),
        ((1, hidden, 9 * channels), bf16),
    ]
    ways = (coils, coils, slabs, pieces, slabs, pieces, pieces, coils, coils)
    changes = pl.pallas_call(
        step_kernel,
        out_shape=jax.ShapeDtypeStruct((3, 2, rows, depth), f32),
        in_specs=[vmem] * 27,
        out_specs=vmem,
        scratch_shapes=[pltpu.VMEM(shape, kind) for shape, kind in buffers]
        + [pltpu.SemaphoreType.DMA((size,)) for size in ways for _ in range(2)],
        compiler_params=pltpu.CompilerParams(collective_id=0, has_side_effects=True),
    )(coil_maps, kspace, sample_mask, iterate, probe_bits, adjoint, *tables, *smalls, *constants)
    changes = changes[:, :, None]
    sign = (2 * probe_bits - 1).astype(f32)
    return iterate + changes[0], sign + changes[1], loss_gradient + (adjoint + changes[2])


def solution(mesh):
    split_coils = P("coil", None, "slab", None, None)
    image = P(None, "slab", "coil", None)
    return jax.shard_map(
        on_device,
        mesh=mesh,
        in_specs=(split_coils, split_coils, P(), image, image, image, image, P(), P(), P()),
        out_specs=(image, image, image),
        check_vma=False,
    )
```

profile of v0, /device:TPU:0, one launch (start us, length us, event | category | flops | bytes accessed | tf_op | source)
XLA Modules:
  0.0 56.1 jit_solution(12627483207706502859)
XLA Ops:
  0.6 0.9 %reverse_bitcast_fusion = bf16[3,3,24,3,24]{2,4,3,0,1:T(8,128)(2,1)S(1)} fusion(bf16[24,24,3,3,3]{1,0,4,3,2:T(8,128)(2,1)} %param.33), kind=kLoop, calls=%fused_computation | loop fusion | bytes 62208 | tf_op jit(solution)/shard_map/transpose;transpose | solution.py:158
  1.6 0.2 copy.59
  1.7 0.0 copy-start
  1.8 0.8 %reshape.37.rest_12_ = bf16[216,72]{1,0:T(8,128)(2,1)} reshape(bf16[3,3,24,3,24]{4,3,2,1,0:T(4,128)(2,1)S(1)} %copy.59) | data formatting | bytes 62208 | tf_op jit(solution)/shard_map/reshape | solution.py:158
  2.5 0.1 copy-done
  2.7 0.1 copy.58
  2.8 0.0 copy-start.5
  2.8 0.8 %reshape.36.rest_9_ = bf16[216,72]{1,0:T(8,128)(2,1)} reshape(bf16[3,3,24,3,24]{4,3,2,1,0:T(4,128)(2,1)S(1)} %copy.58) | data formatting | bytes 62208 | tf_op jit(solution)/shard_map/reshape | solution.py:158
  3.5 0.0 copy-done.5
  3.6 0.1 reshape.35
  3.7 0.0 copy-start.6
  3.7 0.7 %copy.50.rest_13_ = bf16[72,18]{1,0:T(8,128)(2,1)} copy(bf16[72,18]{0,1:T(8,128)(2,1)S(1)} %reshape.35) | data formatting | bytes 5184 | tf_op jit(solution)/shard_map/reshape | solution.py:158
  4.4 0.0 copy-done.6
  4.4 0.1 reshape.30
  4.5 0.7 %copy.47.rest_8_ = bf16[72,18]{1,0:T(8,128)(2,1)} copy(bf16[72,18]{0,1:T(8,128)(2,1)S(1)} %reshape.30) | data formatting | bytes 5184 | tf_op jit(solution)/shard_map/reshape | solution.py:158
  5.2 0.6 %reshape.33.rest_11_ = bf16[54,24]{1,0:T(8,128)(2,1)} reshape(bf16[3,3,3,2,24]{4,3,2,1,0:T(2,128)(2,1)S(1)} %copy.44) | data formatting | bytes 5184 | tf_op jit(solution)/shard_map/reshape | solution.py:158
  5.9 0.6 %reshape.32.rest_10_ = bf16[54,24]{1,0:T(8,128)(2,1)} reshape(bf16[3,3,3,2,24]{4,3,2,1,0:T(2,128)(2,1)S(1)} %copy.43) | data formatting | bytes 5184 | tf_op jit(solution)/shard_map/reshape | solution.py:158
  6.5 0.0 copy-start.1
  6.5 0.0 copy-start.2
  6.5 0.0 copy-start.3
  6.5 0.0 copy-start.4
  6.5 47.9 %shard_map.256 = f32[3,2,64,128]{3,2,1,0:T(8,128)} custom-call(f32[2,2,1,256,128]{4,3,2,1,0:T(8,128)} %maps.1, f32[2,2,1,256,128]{4,3,2,1,0:T(8,128)} %kspace.1, s32[256,128]{1,0:T(8,128)} %mask.1, f32[2,1,64,128]{3,2,1,0:T(8,128)} %iterate.1, s32[2,1,64,128]{3,2,1,0:T(8,128)} %probe_bits.1, f32[2,1,64,128]{3,2,1,0:T(8,128)} %adjoint.1, ...), custom_call_target="tpu_custom_call" | custom-call | tf_op jit(solution)/shard_map/pallas_call | solution.py:460
  54.5 0.0 copy-done.1
  54.5 0.0 copy-done.2
  54.5 0.0 copy-done.3
  54.5 0.0 copy-done.4
  54.5 1.6 %fusion.1 = (f32[2,1,64,128]{3,2,1,0:T(8,128)}, f32[2,1,64,128]{3,2,1,0:T(8,128)}, f32[2,1,64,128]{3,2,1,0:T(8,128)}) fusion(f32[2,1,64,128]{3,2,1,0:T(8,128)S(1)} %copy-done.1, f32[2,1,64,128]{3,2,1,0:T(8,128)S(1)} %copy-done.4, f32[3,2,64,128]{3,2,1,0:T(8,128)} %shard_map.256, s32[2,1,64,128]{3,2,1,0:T(8,128)S(1)} %copy-done.3, ...), kind=kLoop, calls=%fused_computation.3 | loop fusion | flops 114688 | bytes 655360
  (6 shorter events, 0.1 us)
Async XLA Ops:
  1.7 0.9 %copy-start = (bf16[24,24,3,3,3]{1,0,4,3,2:T(8,128)(2,1)S(1)}, bf16[24,24,3,3,3]{1,0,4,3,2:T(8,128)(2,1)}, u32[]{:S(2)}) copy-start(bf16[24,24,3,3,3]{1,0,4,3,2:T(8,128)(2,1)} %param.33) | copy-start | bytes 93316
  2.8 0.8 %copy-start.5 = (bf16[2,24,3,3,3]{1,0,4,3,2:T(2,128)(2,1)S(1)}, bf16[2,24,3,3,3]{1,0,4,3,2:T(2,128)(2,1)}, u32[]{:S(2)}) copy-start(bf16[2,24,3,3,3]{1,0,4,3,2:T(2,128)(2,1)} %param.34) | copy-start | bytes 7780
  3.7 0.7 %copy-start.6 = (bf16[24,2,3,3,3]{0,1,4,3,2:T(2,128)(2,1)S(1)}, bf16[24,2,3,3,3]{0,1,4,3,2:T(2,128)(2,1)}, u32[]{:S(2)}) copy-start(bf16[24,2,3,3,3]{0,1,4,3,2:T(2,128)(2,1)} %param.32) | copy-start | bytes 7780
  6.5 48.0 %copy-start.1 = (f32[2,1,64,128]{3,2,1,0:T(8,128)S(1)}, f32[2,1,64,128]{3,2,1,0:T(8,128)}, u32[]{:S(2)}) copy-start(f32[2,1,64,128]{3,2,1,0:T(8,128)} %adjoint.1) | copy-start | bytes 196612
  6.5 48.0 %copy-start.2 = (f32[2,1,64,128]{3,2,1,0:T(8,128)S(1)}, f32[2,1,64,128]{3,2,1,0:T(8,128)}, u32[]{:S(2)}) copy-start(f32[2,1,64,128]{3,2,1,0:T(8,128)} %iterate.1) | copy-start | bytes 196612
  6.5 48.0 %copy-start.3 = (s32[2,1,64,128]{3,2,1,0:T(8,128)S(1)}, s32[2,1,64,128]{3,2,1,0:T(8,128)}, u32[]{:S(2)}) copy-start(s32[2,1,64,128]{3,2,1,0:T(8,128)} %probe_bits.1) | copy-start | bytes 196612
  6.5 48.0 %copy-start.4 = (f32[2,1,64,128]{3,2,1,0:T(8,128)S(1)}, f32[2,1,64,128]{3,2,1,0:T(8,128)}, u32[]{:S(2)}) copy-start(f32[2,1,64,128]{3,2,1,0:T(8,128)} %param.30) | copy-start | bytes 196612
where the time goes:
time: 56.4 us; the launch traced here: 56.1 us
  Pallas kernels  47.9 us (85%)
  local copies, waits for them, and re-layouts  5.82 us (10%)
  other arithmetic  1.59 us (3%)
  between operations  0.74 us (1%)
    pallas_call x1, Pallas kernels, on_device(): pl.pallas_call(step_kernel, out_shape=jax.ShapeDtypeStruct((3, 2, rows, d...  47.9 us
    reshape x10, local copies, waits for them, and re-layouts, small_kernel(): return jnp.transpose(kernel, order).reshape(taps * 3 * outs, units * ins)  4.66 us
    unnamed x1, other arithmetic  1.59 us

commit v1 on v0

v1 whole, which is shorter than its diff:
```python
import jax
import jax.numpy as jnp
import numpy as np
from jax import lax
from jax.experimental import pallas as pl
from jax.experimental.pallas import tpu as pltpu
from jax.sharding import PartitionSpec as P

step_size = 0.8
reach = 4
f32 = jnp.float32
bf16 = jnp.bfloat16
in_hbm = pl.BlockSpec(memory_space=pltpu.HBM)
anywhere = pl.BlockSpec(memory_space=pl.ANY)
MESH = pl.DeviceIdType.MESH


class Channel:
    def __init__(self, axis, how, source, target, send_sem, recv_sem):
        self.axis, self.how, self.source, self.target = axis, how, source, target
        self.send_sem, self.recv_sem = send_sem, recv_sem
        self.size, self.mine = lax.axis_size(axis), lax.axis_index(axis)

    def row(self, rank):
        return self.source if self.how == "all" else self.source.at[rank]

    def copy(self, source_rank, target_row, device_rank, step):
        return pltpu.make_async_remote_copy(
            src_ref=self.row(source_rank),
            dst_ref=self.target.at[target_row],
            send_sem=self.send_sem.at[step],
            recv_sem=self.recv_sem.at[step],
            device_id=place_of(self.axis, device_rank),
            device_id_type=MESH,
        )

    def start(self):
        for step in range(1, self.size):
            rank = lax.rem(self.mine + step, self.size)
            self.copy(rank, self.mine, rank, step).start()

    def finish(self):
        for step in range(1, self.size):
            rank = lax.rem(self.mine + self.size - step, self.size)
            self.copy(self.mine, rank, rank, step).wait()


def place_of(axis, rank):
    if axis == "coil":
        return rank, lax.axis_index("slab")
    return lax.axis_index("coil"), rank


def greet():
    barrier = pltpu.get_barrier_semaphore()
    count = 0
    for axis in ("coil", "slab"):
        size = lax.axis_size(axis)
        for step in range(1, size):
            rank = lax.rem(lax.axis_index(axis) + step, size)
            pl.semaphore_signal(
                barrier, inc=1, device_id=place_of(axis, rank), device_id_type=MESH
            )
            count += 1
    return barrier, count


def high_low(table):
    high = np.asarray(table, np.float32).astype(jnp.bfloat16)
    return high, (np.asarray(table, np.float32) - high.astype(np.float32)).astype(jnp.bfloat16)


def fourier_tables(height, depth):
    def parts(length):
        counter = np.arange(length)
        angles = (counter[:, None] * counter[None, :] % length) * (2.0 * np.pi / length)
        return np.cos(angles) / np.sqrt(length), np.sin(angles) / np.sqrt(length)

    cos, sin = parts(depth)
    forward = np.block([[cos, -sin], [sin, cos]])
    backward = np.block([[cos, sin], [-sin, cos]])
    return high_low(forward) + high_low(backward) + high_low(np.concatenate(parts(height)))


def groups_of(slices, hidden):
    per = hidden // slices
    out = 4 if slices % 4 == 0 else slices
    spans = []
    for first in range(0, slices, out):
        low = max(first - 1, 0) * per // 32 * 32
        high = min(first + out + 1, slices) * per
        spans.append((low, high))
    width = -(-max(high - low for low, high in spans) // 128) * 128
    if width >= hidden:
        return slices, [0], hidden
    return out, [min(low, hidden - width) for low, _ in spans], width


def mid_eye(hidden, slices, start, width):
    lanes = start + np.arange(width)
    return np.arange(hidden // slices)[:, None] == lanes[None, :] % (hidden // slices)


def pack_constants(height, depth, slices, hidden, channels):
    outs, ins = hidden // slices, channels // slices
    _, starts, width = groups_of(slices, hidden)
    taps = 9
    rows = np.arange(taps * slices * ins)
    row_slice, row_part, row_tap = rows // ins % slices, rows % ins, rows // (slices * ins)
    lane_slice = np.arange(hidden) // outs
    items = {
        "eye": np.eye(outs),
        "spread": np.kron(np.eye(taps), np.tile(np.eye(ins), (1, slices))),
        "tile": np.tile(np.eye(outs), (1, slices)),
    }
    for index, start in enumerate(starts):
        items["mid", index] = mid_eye(hidden, slices, start, width)
    for flip in range(2):
        tap = taps - 1 - row_tap if flip else row_tap
        items["repeat", flip] = (
            np.arange(taps * ins)[None, :] == (tap * ins + row_part)[:, None]
        )
    for dx in range(3):
        items["band", dx] = lane_slice[None, :] == row_slice[:, None] + dx - 1
    names = ("ahead", "ahead_low", "back", "back_low", "down", "down_low")
    items.update(zip(names, fourier_tables(height, depth)))
    lanes = -(-max(item.shape[1] for item in items.values()) // 128) * 128
    places, blocks, at = {}, [], 0
    for name, item in items.items():
        count = -(-item.shape[0] // 16) * 16
        block = np.zeros((count, lanes), jnp.bfloat16)
        block[: item.shape[0], : item.shape[1]] = np.asarray(item).astype(jnp.bfloat16)
        places[name] = (at, item.shape)
        blocks.append(block)
        at += count
    return np.concatenate(blocks), places


def dot(left, right):
    return jnp.dot(left, right, preferred_element_type=f32)


def dot_nt(left, right):
    return lax.dot_general(left, right, (((1,), (1,)), ((), ())), preferred_element_type=f32)


def halves(values):
    high = values.astype(bf16)
    return high, (values - high.astype(f32)).astype(bf16)


def spectrum(values, get, inverse):
    height, depth = values.shape[0], values.shape[1] // 2
    names = ("back", "back_low") if inverse else ("ahead", "ahead_low")
    along_high, along_low = get(names[0]), get(names[1])
    down_high, down_low = get("down"), get("down_low")
    high, low = halves(values)
    high, low = halves(dot(high, along_high) + (dot(low, along_high) + dot(high, along_low)))
    both_parts = dot(down_high, high) + (dot(down_high, low) + dot(down_low, high))
    upper, lower = both_parts[:height], both_parts[height:]
    if inverse:
        return upper[:, :depth] - lower[:, depth:], lower[:, :depth] + upper[:, depth:]
    return upper[:, :depth] + lower[:, depth:], upper[:, depth:] - lower[:, :depth]


def coil_term(real, imag, coil, maps, kspace, mask, get):
    map_real, map_imag = maps[coil, 0, 0], maps[coil, 1, 0]
    image = jnp.concatenate(
        [map_real * real - map_imag * imag, map_real * imag + map_imag * real], axis=1
    )
    freq_real, freq_imag = spectrum(image, get, False)
    if kspace is not None:
        freq_real, freq_imag = freq_real - kspace[coil, 0, 0], freq_imag - kspace[coil, 1, 0]
    freq = jnp.concatenate([mask * freq_real, mask * freq_imag], axis=1)
    back_real, back_imag = spectrum(freq, get, True)
    return (
        map_real * back_real + map_imag * back_imag,
        map_real * back_imag - map_imag * back_real,
    )


def normal_part(real, imag, maps, kspace, mask, get):
    total = None
    for coil in range(maps.shape[0]):
        term = coil_term(real, imag, coil, maps, kspace, mask, get)
        total = term if total is None else (total[0] + term[0], total[1] + term[1])
    return total


def build_in(flat, flip, get, target, slices):
    outs = flat.shape[2]
    lane = lax.broadcasted_iota(jnp.int32, (outs, target.shape[1]), 1).astype(f32)
    ins = target.shape[1] // (9 * slices)
    lane_slice = jnp.floor((lane + 0.5) * (1.0 / ins))
    lane_slice = lane_slice - slices * jnp.floor((lane_slice + 0.5) * (1.0 / slices))
    wide = []
    for dx in range(3):
        turned = dot_nt(get("eye"), flat[2 - dx if flip else dx].astype(bf16)).astype(bf16)
        wide.append(dot(turned, get("spread")))
    for out_slice in range(slices):
        block = None
        for dx in range(3):
            term = jnp.where(lane_slice == float(out_slice + dx - 1), wide[dx], 0.0)
            block = term if block is None else block + term
        target[out_slice * outs : (out_slice + 1) * outs] = block.astype(bf16)


def build_out(flat, flip, get, target):
    total = None
    for dx in range(3):
        wide = dot(flat[2 - dx if flip else dx].astype(bf16), get("tile")).astype(bf16)
        term = dot(get(("repeat", flip)), wide) * get(("band", dx)).astype(f32)
        total = term if total is None else total + term
    target[...] = total.astype(bf16)


def build_mid(raw, flip, get, target, slices):
    outs, hidden = raw.shape[3], target.shape[0] * target.shape[1]
    out_count, starts, width = groups_of(slices, hidden)
    blocks = []
    for dx in range(3):
        for dy in range(3):
            for dz in range(3):
                if flip:
                    blocks.append(dot_nt(get("eye"), raw[2 - dx, 2 - dy, 2 - dz]))
                else:
                    blocks.append(raw[dx, dy, dz].astype(f32))
    stacked = jnp.concatenate(blocks, axis=0).astype(bf16)
    for index, start in enumerate(starts):
        wide = dot(stacked, get(("mid", index)))
        lane = lax.broadcasted_iota(jnp.int32, (outs, width), 1).astype(f32) + float(start)
        lane_slice = jnp.floor((lane + 0.5) * (1.0 / outs))
        for out_at in range(out_count):
            out_slice = index * out_count + out_at
            keeps = [lane_slice == float(out_slice + dx - 1) for dx in range(3)]
            for tap in range(9):
                block = None
                for dx in range(3):
                    at = (dx * 9 + tap) * outs
                    term = jnp.where(keeps[dx], wide[at : at + outs], 0.0)
                    block = term if block is None else block + term
                target[
                    index, out_at * outs : (out_at + 1) * outs, tap * width : (tap + 1) * width
                ] = block.astype(bf16)


def shifted(values, tap, depth):
    if tap == 1:
        return values
    lane = lax.broadcasted_iota(jnp.int32, (values.shape[0], depth), 1)
    edge, turn = (0, 1) if tap == 0 else (depth - 1, depth - 1)
    pieces = []
    for start in range(0, values.shape[1], depth):
        turned = pltpu.roll(values[:, start : start + depth], turn, 1)
        pieces.append(jnp.where(lane == edge, 0.0, turned))
    return jnp.concatenate(pieces, axis=1)


def conv_in(values, weights, depth):
    width = values.shape[1] - 2 * depth
    turned = [shifted(values, tap, depth) for tap in range(3)]
    stacked = jnp.concatenate(
        [turned[dz][:, dy * depth : dy * depth + width] for dy in range(3) for dz in range(3)],
        axis=0,
    )
    return dot(weights[...], stacked.astype(bf16))


def conv_mid(values, weights, depth, slices):
    cols = values.shape[1] - 2 * depth
    _, starts, width = groups_of(slices, values.shape[0])
    turned = [shifted(values, tap, depth).astype(bf16) for tap in range(3)]
    totals = []
    for index, start in enumerate(starts):
        stacked = jnp.concatenate(
            [
                turned[dz][start : start + width, dy * depth : dy * depth + cols]
                for dy in range(3)
                for dz in range(3)
            ],
            axis=0,
        )
        totals.append(dot(weights[index], stacked))
    return jnp.concatenate(totals, axis=0)


def conv_out(values, weights, depth):
    width = values.shape[1] - 2 * depth
    rows = weights.shape[0] // 9
    products = dot(weights[...], values.astype(bf16))
    total = None
    for dz in range(3):
        summed = None
        for dy in range(3):
            at = (dy * 3 + dz) * rows
            term = products[at : at + rows, dy * depth : dy * depth + width]
            summed = term if summed is None else summed + term
        term = shifted(summed, dz, depth)
        total = term if total is None else total + term
    return total


def step_kernel(places, *refs):
    (maps_in, kspace_in, mask_in, iterate_in, bits_in, loss_in, adjoint_in, first_in, second_in,
     last_in, table_in, new_out, probe_out, next_out, *refs) = refs
    (maps, kspace, mask, iterate, bits, loss, adjoint, raw_first, raw_second, raw_last, table,
     load_sem, *refs) = refs
    (outs, out_sem, padded, padded_iterate, padded_fields, padded_relaxed, flats, work, rows_work,
     own_iterate, own_fields, all_iterate, halo, parts_send, parts, window_send, windows,
     fields_send, fields, delta_send, delta, grads_send, grads_back, own_pulled, all_pulled,
     sums_send, sums, first, second, last, first_t, second_t, last_t, halo_sem, *sems) = refs
    channels = []
    for index, (axis, how, source, target) in enumerate((
        ("coil", "all", own_iterate, all_iterate),
        ("slab", "row", fields_send, fields),
        ("coil", "row", parts_send, parts),
        ("slab", "row", window_send, windows),
        ("slab", "row", delta_send, delta),
        ("slab", "row", grads_send.at[0], grads_back.at[0]),
        ("slab", "row", grads_send.at[1], grads_back.at[1]),
        ("coil", "all", own_pulled.at[0], all_pulled.at[0]),
        ("coil", "all", own_pulled.at[1], all_pulled.at[1]),
        ("coil", "row", sums_send.at[0], sums.at[0]),
        ("coil", "row", sums_send.at[1], sums.at[1]),
    )):
        channels.append(Channel(axis, how, source, target, sems[2 * index], sems[2 * index + 1]))
    (iterate_way, field_way, part_way, window_way, delta_way, *later) = channels
    grad_ways, pulled_ways, sum_ways = later[:2], later[2:4], later[4:]

    height, depth = mask.shape
    coils, _, rows, _ = all_iterate.shape
    slices, _, window, _ = windows.shape
    own = window - 2 * reach
    block = rows + 2 * reach
    my_coil, my_slab = lax.axis_index("coil"), lax.axis_index("slab")
    row_base = (my_coil * slices + my_slab) * own - reach
    coil_base = pl.multiple_of(my_coil * rows, 8)

    def get(name):
        at, shape = places[name]
        return table[at : at + shape[0], 0 : shape[1]]

    loads = {}
    tables_at = places["ahead"][0]
    for index, (name, source, target) in enumerate((
        ("iterate", iterate_in, iterate),
        ("bits", bits_in, bits),
        ("adjoint", adjoint_in, adjoint),
        ("second", second_in, raw_second),
        ("first", first_in, raw_first),
        ("last", last_in, raw_last),
        ("small", table_in.at[0:tables_at], table.at[0:tables_at]),
        ("maps", maps_in, maps),
        ("tables", table_in.at[tables_at:], table.at[tables_at:]),
        ("mask", mask_in, mask),
        ("kspace", kspace_in, kspace),
        ("loss", loss_in, loss),
    )):
        loads[name] = pltpu.make_async_copy(source, target, load_sem.at[index])
    barrier, arrivals = greet()
    for load in loads.values():
        load.start()
    edge = jnp.zeros((2, 8, depth), f32)
    for target in (padded, padded_iterate):
        target[:, 0:8] = edge
        target[:, height + reach : height + reach + 8] = edge
    loads["iterate"].wait()
    own_iterate[...] = iterate[:, 0].astype(bf16)
    pl.semaphore_wait(barrier, arrivals)
    iterate_way.start()
    loads["bits"].wait()
    loads["adjoint"].wait()
    own_fields[0:2] = (2 * bits[:, 0] - 1).astype(bf16)
    own_fields[2:4] = adjoint[:, 0].astype(bf16)
    halo_ways = []
    for side, (turn, at) in enumerate(((1, rows - 8), (coils - 1, 0))):
        halo_ways.append(
            pltpu.make_async_remote_copy(
                src_ref=own_fields.at[:, at : at + 8],
                dst_ref=halo.at[side],
                send_sem=halo_sem.at[side],
                recv_sem=halo_sem.at[2 + side],
                device_id=place_of("coil", lax.rem(my_coil + turn, coils)),
                device_id_type=MESH,
            )
        )
        halo_ways[-1].start()
    padded_fields[:, reach : reach + rows] = own_fields[...].astype(f32)
    for name in ("second", "first", "last", "small"):
        loads[name].wait()
    for side, raw in enumerate((raw_first, raw_last)):
        for dx in range(3):
            for tap in range(9):
                parts_of = raw[dx, tap // 3, tap % 3].astype(f32)
                flats[2 * side, dx, 2 * tap : 2 * tap + 2] = parts_of
                flats[2 * side + 1, dx, 16 - 2 * tap : 18 - 2 * tap] = parts_of
    build_in(flats.at[3], 1, get, last_t, slices)
    build_in(flats.at[0], 0, get, first, slices)
    build_mid(raw_second, 0, get, second, slices)
    build_mid(raw_second, 1, get, second_t, slices)
    build_out(flats.at[2], 0, get, last)
    build_out(flats.at[0], 1, get, first_t)
    for way in halo_ways:
        way.wait()
    keep = jnp.where(my_coil > 0, 1.0, 0.0).astype(f32)
    padded_fields[:, 0:reach] = halo[0, :, 8 - reach : 8].astype(f32) * keep
    keep = jnp.where(my_coil < coils - 1, 1.0, 0.0).astype(f32)
    padded_fields[:, reach + rows : block] = halo[1, :, 0:reach].astype(f32) * keep
    for piece in range(slices):
        fields_send[piece] = padded_fields[:, piece * own : piece * own + window].astype(bf16)
    field_way.start()
    for name in ("maps", "tables", "mask", "kspace"):
        loads[name].wait()
    weight = mask[...].astype(f32)
    all_iterate[my_coil] = own_iterate[...]
    iterate_way.finish()

    def column(gathered, channel):
        return jnp.concatenate(
            [gathered[piece, channel].astype(f32) for piece in range(coils)], axis=0
        )

    real, imag = column(all_iterate, 0), column(all_iterate, 1)
    total = normal_part(real, imag, maps, kspace, weight, get)
    padded[0, reach : reach + height] = total[0]
    padded[1, reach : reach + height] = total[1]
    for piece in range(coils):
        parts_send[piece] = padded[:, piece * rows : piece * rows + block].astype(bf16)
    part_way.start()
    padded_iterate[0, reach : reach + height] = real
    padded_iterate[1, reach : reach + height] = imag
    padded_relaxed[:, 0:block] = padded_iterate[:, pl.ds(coil_base, block)]
    padded_relaxed[:, reach : reach + rows] = iterate[:, 0]

    def load(values):
        work[...] = values.astype(f32).reshape(work.shape)
        return jnp.concatenate([work[:, row, :] for row in range(window)], axis=1)

    def cut(values, before, after):
        return values[:, before * depth : values.shape[1] - after * depth]

    def inside(values, offset):
        blocks = []
        for row in range(values.shape[1] // depth):
            at = row_base + offset + row
            keep = jnp.where((at >= 0) & (at < height), 1.0, 0.0).astype(f32)
            blocks.append(values[:, row * depth : (row + 1) * depth] * keep)
        return jnp.concatenate(blocks, axis=1)

    def store(values):
        for row in range(own):
            rows_work[:, row, :] = values[:, row * depth : (row + 1) * depth]
        return rows_work[...].reshape(slices, 2, own, depth).astype(bf16)

    fields[my_slab] = fields_send[my_slab]
    field_way.finish()
    grads = []
    for field in range(2):
        probe = cut(load(fields[:, 2 * field : 2 * field + 2]), 1, 1)
        grads.append(conv_in(probe, last_t, depth))
    part_way.finish()
    summed = padded[:, pl.ds(coil_base, block)]
    for step in range(1, coils):
        summed = summed + parts[lax.rem(my_coil + step, coils)].astype(f32)
    padded_relaxed[:, 0:block] = padded_relaxed[:, 0:block] - step_size * summed
    for piece in range(slices):
        window_send[piece] = padded_relaxed[:, piece * own : piece * own + window].astype(bf16)
    window_way.start()
    windows[my_slab] = window_send[my_slab]
    window_way.finish()

    pre1 = conv_in(load(windows[...]), first, depth)
    sig1 = jax.nn.sigmoid(pre1)
    act1 = inside(pre1 * sig1, 1)
    slope1 = inside(cut(sig1 * (1.0 + pre1 * (1.0 - sig1)), 2, 2), 3)
    pre2 = conv_mid(act1, second, depth, slices)
    sig2 = jax.nn.sigmoid(pre2)
    slope2 = inside(sig2 * (1.0 + pre2 * (1.0 - sig2)), 2)
    for field in range(2):
        grad1 = conv_mid(grads[field] * slope2, second_t, depth, slices) * slope1
        grads_send[field] = store(conv_out(grad1, first_t, depth))
        grad_ways[field].start()
        grads_back[field, my_slab] = grads_send[field, my_slab]
    act2 = inside(cut(pre2 * sig2, 1, 1), 3)
    delta_out = store(conv_out(act2, last, depth))

    exact = ((2 * bits[:, 0] - 1).astype(f32), adjoint[:, 0])
    pulled = []
    for field in range(2):
        grad_ways[field].finish()
        back = jnp.concatenate(
            [grads_back[field, piece].astype(f32) for piece in range(slices)], axis=1
        )
        pulled.append(exact[field] + back)
        own_pulled[field] = pulled[field].astype(bf16)
        pulled_ways[field].start()
        all_pulled[field, my_coil] = own_pulled[field]
        if field == 0:
            delta_send[...] = delta_out
            delta_way.start()
            delta[my_slab] = delta_send[my_slab]
    partial = []
    for field in range(2):
        pulled_ways[field].finish()
        real, imag = column(all_pulled.at[field], 0), column(all_pulled.at[field], 1)
        total = normal_part(real, imag, maps, None, weight, get)
        for part in range(2):
            padded[part, 0:height] = total[part]
            for piece in range(coils):
                sums_send[field, piece, part] = total[part][
                    piece * rows : (piece + 1) * rows
                ].astype(bf16)
        sum_ways[field].start()
        partial.append(padded[:, pl.ds(coil_base, rows)])

    results = (new_out, probe_out, next_out)
    finals = [
        pltpu.make_async_copy(outs.at[index], results[index], out_sem.at[index])
        for index in range(3)
    ]
    delta_way.finish()
    for piece in range(slices):
        at = piece * own
        outs[0, :, 0, at : at + own] = (
            padded_relaxed[:, reach + at : reach + at + own] + delta[piece].astype(f32)
        )
    finals[0].start()
    loads["loss"].wait()
    for field in range(2):
        sum_ways[field].finish()
        added = partial[field]
        for step in range(1, coils):
            added = added + sums[field, lax.rem(my_coil + step, coils)].astype(f32)
        value = pulled[field] - step_size * added
        outs[1 + field, :, 0] = value if field == 0 else loss[:, 0] + value
        finals[1 + field].start()
    for final in finals:
        final.wait()


def on_device(coil_maps, kspace, sample_mask, iterate, probe_bits, loss_gradient, adjoint,
              kernel_first, kernel_second, kernel_last):
    height, depth = sample_mask.shape
    coils, slabs = lax.axis_size("coil"), lax.axis_size("slab")
    own = height // (coils * slabs)
    window = own + 2 * reach
    rows = iterate.shape[2]
    block = rows + 2 * reach
    hidden, channels = kernel_second.shape[0] * slabs, kernel_first.shape[1] * slabs
    table, places = pack_constants(height, depth, slabs, hidden, channels)
    raws = (
        jnp.transpose(kernel_first, (2, 3, 4, 1, 0)),
        jnp.transpose(kernel_second, (2, 3, 4, 0, 1)),
        jnp.transpose(kernel_last, (2, 3, 4, 0, 1)),
    )
    operands = (coil_maps, kspace, sample_mask, iterate, probe_bits, loss_gradient, adjoint, *raws,
                jnp.asarray(table))
    _, starts, width = groups_of(slabs, hidden)
    mids = (len(starts), hidden // len(starts), 9 * width)
    image = jax.ShapeDtypeStruct(iterate.shape, f32)
    buffers = [
        ((2, height + 2 * reach + 8, depth), f32),
        ((2, height + 2 * reach + 8, depth), f32),
        ((4, block + 8, depth), f32),
        ((2, block + 8, depth), f32),
        ((4, 3, 18, kernel_second.shape[0]), f32),
        ((2 * slabs, window, depth), f32),
        ((2 * slabs, own, depth), f32),
        ((2, rows, depth), bf16),
        ((4, rows, depth), bf16),
        ((coils, 2, rows, depth), bf16),
        ((2, 4, 8, depth), bf16),
        ((coils, 2, block, depth), bf16),
        ((coils, 2, block, depth), bf16),
        ((slabs, 2, window, depth), bf16),
        ((slabs, 2, window, depth), bf16),
        ((slabs, 4, window, depth), bf16),
        ((slabs, 4, window, depth), bf16),
        ((slabs, 2, own, depth), bf16),
        ((slabs, 2, own, depth), bf16),
        ((2, slabs, 2, own, depth), bf16),
        ((2, slabs, 2, own, depth), bf16),
        ((2, 2, rows, depth), bf16),
        ((2, coils, 2, rows, depth), bf16),
        ((2, coils, 2, rows, depth), bf16),
        ((2, coils, 2, rows, depth), bf16),
        ((hidden, 9 * channels), bf16),
        (mids, bf16),
        ((9 * channels, hidden), bf16),
        ((9 * channels, hidden), bf16),
        (mids, bf16),
        ((hidden, 9 * channels), bf16),
    ]
    ways = (coils, slabs, coils, slabs, slabs, slabs, slabs, coils, coils, coils, coils)
    return pl.pallas_call(
        lambda *refs: step_kernel(places, *refs),
        out_shape=(image, image, image),
        in_specs=[in_hbm] * len(operands),
        out_specs=(anywhere,) * 3,
        scratch_shapes=[pltpu.VMEM(value.shape, value.dtype) for value in operands]
        + [pltpu.SemaphoreType.DMA((12,)), pltpu.VMEM((3, *iterate.shape), f32)]
        + [pltpu.SemaphoreType.DMA((3,))]
        + [pltpu.VMEM(shape, kind) for shape, kind in buffers]
        + [pltpu.SemaphoreType.DMA((4,))]
        + [pltpu.SemaphoreType.DMA((size,)) for size in ways for _ in range(2)],
        compiler_params=pltpu.CompilerParams(
            collective_id=0, has_side_effects=True, vmem_limit_bytes=66_800_000
        ),
        name="step",
    )(*operands)


def solution(mesh):
    split_coils = P("coil", None, "slab", None, None)
    image = P(None, "slab", "coil", None)
    return jax.shard_map(
        on_device,
        mesh=mesh,
        in_specs=(split_coils, split_coils, P(), image, image, image, image, P(), P(), P()),
        out_specs=(image, image, image),
        check_vma=False,
    )
```

time: 56.4 us -> 45.7 us (0.81)
  Pallas kernels: 47.9 us -> 40.3 us
  other arithmetic: 1.59 us -> 0 us
  local copies, waits for them, and re-layouts: 5.82 us -> 4.42 us
    pallas_call x1, Pallas kernels: 47.9 us -> 40.3 us  [on_device(): pl.pallas_call(lambda *refs: step_kernel(places, *refs), out_shape=(image...]
    reshape x10 -> x0, local copies, waits for them, and re-layouts: 4.66 us -> none  [small_kernel(): return jnp.transpose(kernel, order).reshape(taps * 3 * outs, units * ins)]
    unnamed x14 -> x3, local copies, waits for them, and re-layouts: 0.16 us -> 4.42 us
    unnamed x1 -> x0, other arithmetic: 1.59 us -> none
    another operation x5 -> x0, local copies, waits for them, and re-layouts: 0.98 us -> none  [small_kernel(): return jnp.transpose(kernel, order).reshape(taps * 3 * outs, units * ins)]
where the time goes in v1:
time: 45.7 us; the launch traced here: 45.4 us
  Pallas kernels  40.3 us (88%)
  local copies, waits for them, and re-layouts  4.42 us (10%)
  between operations  0.64 us (1%)
    pallas_call x1, Pallas kernels, on_device(): pl.pallas_call(lambda *refs: step_kernel(places, *refs), out_shape=(image...  40.3 us
    unnamed x3, local copies, waits for them, and re-layouts  4.42 us

profile of v1, /device:TPU:0, one launch (start us, length us, event | category | flops | bytes accessed | tf_op | source)
XLA Modules:
  0.0 45.4 jit_solution(13996860340382379727)
XLA Ops:
  0.6 40.3 %step.1 = (f32[2,1,64,128]{3,2,1,0:T(8,128)}, f32[2,1,64,128]{3,2,1,0:T(8,128)}, f32[2,1,64,128]{3,2,1,0:T(8,128)}) custom-call(f32[2,2,1,256,128]{4,3,2,1,0:T(8,128)} %refs_0_.1, f32[2,2,1,256,128]{4,3,2,1,0:T(8,128)} %refs_1_.1, s32[256,128]{1,0:T(8,128)} %refs_2_.1, f32[2,1,64,128]{3,2,1,0:T(8,128)} %refs_3_.1, s32[2,1,64,128]{3,2,1,0:T(8,128)} %refs_4_.1, ...), custom_call_target="tpu_custom_call" | custom-call | tf_op jit(solution)/shard_map/step/pallas_call | solution.py:595
  41.0 1.5 %copy.17 = f32[2,1,64,128]{3,2,1,0:T(8,128)} copy(f32[2,1,64,128]{3,2,1,0:T(8,128)} %get-tuple-element.6) | data formatting | bytes 131072
  42.5 1.5 %copy.18 = f32[2,1,64,128]{3,2,1,0:T(8,128)} copy(f32[2,1,64,128]{3,2,1,0:T(8,128)} %get-tuple-element.7) | data formatting | bytes 131072
  43.9 1.5 %copy.19 = f32[2,1,64,128]{3,2,1,0:T(8,128)} copy(f32[2,1,64,128]{3,2,1,0:T(8,128)} %get-tuple-element.8) | data formatting | bytes 131072

commit v2 on v1

--- a/solution.py
+++ b/solution.py
@@ -11,7 +11,7 @@
 f32 = jnp.float32
 bf16 = jnp.bfloat16
 in_hbm = pl.BlockSpec(memory_space=pltpu.HBM)
-anywhere = pl.BlockSpec(memory_space=pl.ANY)
+in_vmem = pl.BlockSpec(memory_space=pltpu.VMEM)
 MESH = pl.DeviceIdType.MESH
 
 
@@ -149,14 +149,17 @@
     return high, (values - high.astype(f32)).astype(bf16)
 
 
-def spectrum(values, get, inverse):
+def spectrum(values, get, inverse, fine):
     height, depth = values.shape[0], values.shape[1] // 2
     names = ("back", "back_low") if inverse else ("ahead", "ahead_low")
-    along_high, along_low = get(names[0]), get(names[1])
-    down_high, down_low = get("down"), get("down_low")
     high, low = halves(values)
-    high, low = halves(dot(high, along_high) + (dot(low, along_high) + dot(high, along_low)))
-    both_parts = dot(down_high, high) + (dot(down_high, low) + dot(down_low, high))
+    turned = dot(high, get(names[0]))
+    if fine:
+        turned = turned + (dot(low, get(names[0])) + dot(high, get(names[1])))
+    high, low = halves(turned)
+    both_parts = dot(get("down"), high)
+    if fine:
+        both_parts = both_parts + (dot(get("down"), low) + dot(get("down_low"), high))
     upper, lower = both_parts[:height], both_parts[height:]
     if inverse:
         return upper[:, :depth] - lower[:, depth:], lower[:, :depth] + upper[:, depth:]
@@ -168,11 +171,11 @@
     image = jnp.concatenate(
         [map_real * real - map_imag * imag, map_real * imag + map_imag * real], axis=1
     )
-    freq_real, freq_imag = spectrum(image, get, False)
+    freq_real, freq_imag = spectrum(image, get, False, False)
     if kspace is not None:
         freq_real, freq_imag = freq_real - kspace[coil, 0, 0], freq_imag - kspace[coil, 1, 0]
     freq = jnp.concatenate([mask * freq_real, mask * freq_imag], axis=1)
-    back_real, back_imag = spectrum(freq, get, True)
+    back_real, back_imag = spectrum(freq, get, True, kspace is not None)
     return (
         map_real * back_real + map_imag * back_imag,
         map_real * back_imag - map_imag * back_real,
@@ -300,12 +303,16 @@
     return total
 
 
+def sigmoid(values):
+    return 0.5 + 0.5 * jnp.tanh(0.5 * values)
+
+
 def step_kernel(places, *refs):
-    (maps_in, kspace_in, mask_in, iterate_in, bits_in, loss_in, adjoint_in, first_in, second_in,
-     last_in, table_in, new_out, probe_out, next_out, *refs) = refs
-    (maps, kspace, mask, iterate, bits, loss, adjoint, raw_first, raw_second, raw_last, table,
+    (maps_in, kspace_in, mask_in, iterate_in, bits_in, adjoint_in, first_in, second_in,
+     last_in, table_in, result, *refs) = refs
+    (maps, kspace, mask, iterate, bits, adjoint, raw_first, raw_second, raw_last, table,
      load_sem, *refs) = refs
-    (outs, out_sem, padded, padded_iterate, padded_fields, padded_relaxed, flats, work, rows_work,
+    (padded, padded_iterate, padded_fields, padded_relaxed, flats, work, rows_work,
      own_iterate, own_fields, all_iterate, halo, parts_send, parts, window_send, windows,
      fields_send, fields, delta_send, delta, grads_send, grads_back, own_pulled, all_pulled,
      sums_send, sums, first, second, last, first_t, second_t, last_t, halo_sem, *sems) = refs
@@ -354,7 +361,6 @@
         ("tables", table_in.at[tables_at:], table.at[tables_at:]),
         ("mask", mask_in, mask),
         ("kspace", kspace_in, kspace),
-        ("loss", loss_in, loss),
     )):
         loads[name] = pltpu.make_async_copy(source, target, load_sem.at[index])
     barrier, arrivals = greet()
@@ -385,7 +391,6 @@
             )
         )
         halo_ways[-1].start()
-    padded_fields[:, reach : reach + rows] = own_fields[...].astype(f32)
     for name in ("second", "first", "last", "small"):
         loads[name].wait()
     for side, raw in enumerate((raw_first, raw_last)):
@@ -398,8 +403,25 @@
     build_in(flats.at[0], 0, get, first, slices)
     build_mid(raw_second, 0, get, second, slices)
     build_mid(raw_second, 1, get, second_t, slices)
-    build_out(flats.at[2], 0, get, last)
-    build_out(flats.at[0], 1, get, first_t)
+    for name in ("maps", "tables", "mask", "kspace"):
+        loads[name].wait()
+    weight = mask[...].astype(f32)
+    all_iterate[my_coil] = own_iterate[...]
+    iterate_way.finish()
+
+    def column(gathered, channel):
+        return jnp.concatenate(
+            [gathered[piece, channel].astype(f32) for piece in range(coils)], axis=0
+        )
+
+    real, imag = column(all_iterate, 0), column(all_iterate, 1)
+    total = normal_part(real, imag, maps, kspace, weight, get)
+    padded[0, reach : reach + height] = total[0]
+    padded[1, reach : reach + height] = total[1]
+    for piece in range(coils):
+        parts_send[piece] = padded[:, piece * rows : piece * rows + block].astype(bf16)
+    part_way.start()
+    padded_fields[:, reach : reach + rows] = own_fields[...].astype(f32)
     for way in halo_ways:
         way.wait()
     keep = jnp.where(my_coil > 0, 1.0, 0.0).astype(f32)
@@ -409,24 +431,6 @@
     for piece in range(slices):
         fields_send[piece] = padded_fields[:, piece * own : piece * own + window].astype(bf16)
     field_way.start()
-    for name in ("maps", "tables", "mask", "kspace"):
-        loads[name].wait()
-    weight = mask[...].astype(f32)
-    all_iterate[my_coil] = own_iterate[...]
-    iterate_way.finish()
-
-    def column(gathered, channel):
-        return jnp.concatenate(
-            [gathered[piece, channel].astype(f32) for piece in range(coils)], axis=0
-        )
-
-    real, imag = column(all_iterate, 0), column(all_iterate, 1)
-    total = normal_part(real, imag, maps, kspace, weight, get)
-    padded[0, reach : reach + height] = total[0]
-    padded[1, reach : reach + height] = total[1]
-    for piece in range(coils):
-        parts_send[piece] = padded[:, piece * rows : piece * rows + block].astype(bf16)
-    part_way.start()
     padded_iterate[0, reach : reach + height] = real
     padded_iterate[1, reach : reach + height] = imag
     padded_relaxed[:, 0:block] = padded_iterate[:, pl.ds(coil_base, block)]
@@ -452,12 +456,8 @@
             rows_work[:, row, :] = values[:, row * depth : (row + 1) * depth]
         return rows_work[...].reshape(slices, 2, own, depth).astype(bf16)
 
-    fields[my_slab] = fields_send[my_slab]
-    field_way.finish()
-    grads = []
-    for field in range(2):
-        probe = cut(load(fields[:, 2 * field : 2 * field + 2]), 1, 1)
-        grads.append(conv_in(probe, last_t, depth))
+    build_out(flats.at[2], 0, get, last)
+    build_out(flats.at[0], 1, get, first_t)
     part_way.finish()
     summed = padded[:, pl.ds(coil_base, block)]
     for step in range(1, coils):
@@ -467,32 +467,40 @@
         window_send[piece] = padded_relaxed[:, piece * own : piece * own + window].astype(bf16)
     window_way.start()
     windows[my_slab] = window_send[my_slab]
+    fields[my_slab] = fields_send[my_slab]
+    field_way.finish()
+    grads = []
+    for field in range(2):
+        probe = cut(load(fields[:, 2 * field : 2 * field + 2]), 1, 1)
+        grads.append(conv_in(probe, last_t, depth))
     window_way.finish()
 
     pre1 = conv_in(load(windows[...]), first, depth)
-    sig1 = jax.nn.sigmoid(pre1)
-    act1 = inside(pre1 * sig1, 1)
-    slope1 = inside(cut(sig1 * (1.0 + pre1 * (1.0 - sig1)), 2, 2), 3)
+    sig1 = sigmoid(pre1)
+    act1 = pre1 * sig1
+    slope1 = inside(cut(sig1 + act1 * (1.0 - sig1), 2, 2), 3)
+    act1 = inside(act1, 1)
     pre2 = conv_mid(act1, second, depth, slices)
-    sig2 = jax.nn.sigmoid(pre2)
-    slope2 = inside(sig2 * (1.0 + pre2 * (1.0 - sig2)), 2)
+    sig2 = sigmoid(pre2)
+    act2 = pre2 * sig2
+    slope2 = inside(sig2 + act2 * (1.0 - sig2), 2)
     for field in range(2):
         grad1 = conv_mid(grads[field] * slope2, second_t, depth, slices) * slope1
         grads_send[field] = store(conv_out(grad1, first_t, depth))
         grad_ways[field].start()
         grads_back[field, my_slab] = grads_send[field, my_slab]
-    act2 = inside(cut(pre2 * sig2, 1, 1), 3)
+    act2 = inside(cut(act2, 1, 1), 3)
     delta_out = store(conv_out(act2, last, depth))
 
     exact = ((2 * bits[:, 0] - 1).astype(f32), adjoint[:, 0])
-    pulled = []
+    backs = []
     for field in range(2):
         grad_ways[field].finish()
         back = jnp.concatenate(
             [grads_back[field, piece].astype(f32) for piece in range(slices)], axis=1
         )
-        pulled.append(exact[field] + back)
-        own_pulled[field] = pulled[field].astype(bf16)
+        backs.append(back)
+        own_pulled[field] = (exact[field] + back).astype(bf16)
         pulled_ways[field].start()
         all_pulled[field, my_coil] = own_pulled[field]
         if field == 0:
@@ -513,29 +521,18 @@
         sum_ways[field].start()
         partial.append(padded[:, pl.ds(coil_base, rows)])
 
-    results = (new_out, probe_out, next_out)
-    finals = [
-        pltpu.make_async_copy(outs.at[index], results[index], out_sem.at[index])
-        for index in range(3)
-    ]
     delta_way.finish()
     for piece in range(slices):
         at = piece * own
-        outs[0, :, 0, at : at + own] = (
-            padded_relaxed[:, reach + at : reach + at + own] + delta[piece].astype(f32)
-        )
-    finals[0].start()
-    loads["loss"].wait()
+        result[0, :, at : at + own] = (
+            padded_relaxed[:, reach + at : reach + at + own] - iterate[:, 0, at : at + own]
+        ) + delta[piece].astype(f32)
     for field in range(2):
         sum_ways[field].finish()
         added = partial[field]
         for step in range(1, coils):
             added = added + sums[field, lax.rem(my_coil + step, coils)].astype(f32)
-        value = pulled[field] - step_size * added
-        outs[1 + field, :, 0] = value if field == 0 else loss[:, 0] + value
-        finals[1 + field].start()
-    for final in finals:
-        final.wait()
+        result[1 + field] = backs[field] - step_size * added
 
 
 def on_device(coil_maps, kspace, sample_mask, iterate, probe_bits, loss_gradient, adjoint,
@@ -553,11 +550,10 @@
         jnp.transpose(kernel_second, (2, 3, 4, 0, 1)),
         jnp.transpose(kernel_last, (2, 3, 4, 0, 1)),
     )
-    operands = (coil_maps, kspace, sample_mask, iterate, probe_bits, loss_gradient, adjoint, *raws,
+    operands = (coil_maps, kspace, sample_mask, iterate, probe_bits, adjoint, *raws,
                 jnp.asarray(table))
     _, starts, width = groups_of(slabs, hidden)
     mids = (len(starts), hidden // len(starts), 9 * width)
-    image = jax.ShapeDtypeStruct(iterate.shape, f32)
     buffers = [
         ((2, height + 2 * reach + 8, depth), f32),
         ((2, height + 2 * reach + 8, depth), f32),
@@ -592,22 +588,24 @@
         ((hidden, 9 * channels), bf16),
     ]
     ways = (coils, slabs, coils, slabs, slabs, slabs, slabs, coils, coils, coils, coils)
-    return pl.pallas_call(
+    changes = pl.pallas_call(
         lambda *refs: step_kernel(places, *refs),
-        out_shape=(image, image, image),
+        out_shape=pltpu.VMEM((3, 2, rows, depth), f32),
         in_specs=[in_hbm] * len(operands),
-        out_specs=(anywhere,) * 3,
+        out_specs=in_vmem,
         scratch_shapes=[pltpu.VMEM(value.shape, value.dtype) for value in operands]
-        + [pltpu.SemaphoreType.DMA((12,)), pltpu.VMEM((3, *iterate.shape), f32)]
-        + [pltpu.SemaphoreType.DMA((3,))]
+        + [pltpu.SemaphoreType.DMA((11,))]
         + [pltpu.VMEM(shape, kind) for shape, kind in buffers]
         + [pltpu.SemaphoreType.DMA((4,))]
         + [pltpu.SemaphoreType.DMA((size,)) for size in ways for _ in range(2)],
         compiler_params=pltpu.CompilerParams(
-            collective_id=0, has_side_effects=True, vmem_limit_bytes=66_800_000
+            collective_id=0, has_side_effects=True, vmem_limit_bytes=40 << 20
         ),
         name="step",
-    )(*operands)
+    )(*[pltpu.with_memory_space_constraint(value, pltpu.HBM) for value in operands])
+    changes = changes[:, :, None]
+    sign = (2 * probe_bits - 1).astype(f32)
+    return iterate + changes[0], sign + changes[1], loss_gradient + (adjoint + changes[2])
 
 
 def solution(mesh):

time: 45.7 us -> 37.9 us (0.83)
  local copies, waits for them, and re-layouts: 4.42 us -> 0.02 us
  Pallas kernels: 40.3 us -> 36.3 us
  other arithmetic: 0 us -> 0.69 us
    unnamed x3 -> x8, local copies, waits for them, and re-layouts: 4.42 us -> 0.02 us
    pallas_call x1, Pallas kernels: 40.3 us -> 36.3 us  [on_device(): pl.pallas_call(lambda *refs: step_kernel(places, *refs), out_shape=pltpu....]
    unnamed x0 -> x1, other arithmetic: none -> 0.69 us
where the time goes in v2:
time: 37.9 us; the launch traced here: 37.8 us
  Pallas kernels  36.3 us (96%)
  between operations  0.71 us (2%)
  other arithmetic  0.69 us (2%)
    pallas_call x1, Pallas kernels, on_device(): pl.pallas_call(lambda *refs: step_kernel(places, *refs), out_shape=pltpu....  36.3 us

profile of v2, /device:TPU:0, one launch (start us, length us, event | category | flops | bytes accessed | tf_op | source)
XLA Modules:
  0.0 37.8 jit_solution(3502450965503487909)
XLA Ops:
  0.6 0.0 copy-start
  0.6 0.0 copy-start.1
  0.7 0.0 copy-start.2
  0.7 0.0 copy-start.3
  0.7 36.3 %step.1 = f32[3,2,64,128]{3,2,1,0:T(8,128)S(1)} custom-call(f32[2,2,1,256,128]{4,3,2,1,0:T(8,128)} %refs_0_.1, f32[2,2,1,256,128]{4,3,2,1,0:T(8,128)} %refs_1_.1, s32[256,128]{1,0:T(8,128)} %refs_2_.1, f32[2,1,64,128]{3,2,1,0:T(8,128)} %refs_3_.1, s32[2,1,64,128]{3,2,1,0:T(8,128)} %refs_4_.1, f32[2,1,64,128]{3,2,1,0:T(8,128)} %refs_5_.1, ...), custom_call_target="tpu_custom_call" | custom-call | tf_op jit(solution)/shard_map/step/pallas_call | solution.py:591
  37.0 0.0 copy-done
  37.0 0.0 copy-done.1
  37.0 0.0 copy-done.2
  37.1 0.0 copy-done.3
  37.1 0.7 %fusion.1 = (f32[2,1,64,128]{3,2,1,0:T(8,128)}, f32[2,1,64,128]{3,2,1,0:T(8,128)}, f32[2,1,64,128]{3,2,1,0:T(8,128)}) fusion(f32[2,1,64,128]{3,2,1,0:T(8,128)S(1)} %copy-done, f32[2,1,64,128]{3,2,1,0:T(8,128)S(1)} %copy-done.3, f32[3,2,64,128]{3,2,1,0:T(8,128)S(1)} %step.1, s32[2,1,64,128]{3,2,1,0:T(8,128)S(1)} %copy-done.2, f32[2,1,64,128]{3,2,1,0:T(8,128)S(1)} %copy-done.1), kind=kLoop, calls=%fused_computation.2 | loop fusion | flops 114688 | bytes 655360
Async XLA Ops:
  0.6 36.4 %copy-start = (f32[2,1,64,128]{3,2,1,0:T(8,128)S(1)}, f32[2,1,64,128]{3,2,1,0:T(8,128)}, u32[]{:S(2)}) copy-start(f32[2,1,64,128]{3,2,1,0:T(8,128)} %refs_5_.1) | copy-start | bytes 196612
  0.6 36.4 %copy-start.1 = (f32[2,1,64,128]{3,2,1,0:T(8,128)S(1)}, f32[2,1,64,128]{3,2,1,0:T(8,128)}, u32[]{:S(2)}) copy-start(f32[2,1,64,128]{3,2,1,0:T(8,128)} %refs_3_.1) | copy-start | bytes 196612
  0.7 36.4 %copy-start.2 = (s32[2,1,64,128]{3,2,1,0:T(8,128)S(1)}, s32[2,1,64,128]{3,2,1,0:T(8,128)}, u32[]{:S(2)}) copy-start(s32[2,1,64,128]{3,2,1,0:T(8,128)} %refs_4_.1) | copy-start | bytes 196612
  0.7 36.4 %copy-start.3 = (f32[2,1,64,128]{3,2,1,0:T(8,128)S(1)}, f32[2,1,64,128]{3,2,1,0:T(8,128)}, u32[]{:S(2)}) copy-start(f32[2,1,64,128]{3,2,1,0:T(8,128)} %param.16) | copy-start | bytes 196612

commit v3 on v2

--- a/solution.py
+++ b/solution.py
@@ -24,12 +24,12 @@
     def row(self, rank):
         return self.source if self.how == "all" else self.source.at[rank]
 
-    def copy(self, source_rank, target_row, device_rank, step):
+    def copy(self, source_rank, target_row, device_rank):
         return pltpu.make_async_remote_copy(
             src_ref=self.row(source_rank),
             dst_ref=self.target.at[target_row],
-            send_sem=self.send_sem.at[step],
-            recv_sem=self.recv_sem.at[step],
+            send_sem=self.send_sem,
+            recv_sem=self.recv_sem,
             device_id=place_of(self.axis, device_rank),
             device_id_type=MESH,
         )
@@ -37,12 +37,12 @@
     def start(self):
         for step in range(1, self.size):
             rank = lax.rem(self.mine + step, self.size)
-            self.copy(rank, self.mine, rank, step).start()
+            self.copy(rank, self.mine, rank).start()
 
     def finish(self):
-        for step in range(1, self.size):
-            rank = lax.rem(self.mine + self.size - step, self.size)
-            self.copy(self.mine, rank, rank, step).wait()
+        landed = self.target.at[0 : self.size - 1]
+        for sem in (self.send_sem, self.recv_sem):
+            pltpu.make_async_copy(landed, landed, sem).wait()
 
 
 def place_of(axis, rank):
@@ -149,43 +149,53 @@
     return high, (values - high.astype(f32)).astype(bf16)
 
 
-def spectrum(values, get, inverse, fine):
-    height, depth = values.shape[0], values.shape[1] // 2
+def spectrum(images, get, inverse, fine):
+    count, height, depth = len(images), images[0].shape[0], images[0].shape[1] // 2
     names = ("back", "back_low") if inverse else ("ahead", "ahead_low")
-    high, low = halves(values)
+    high, low = halves(jnp.concatenate(images, axis=0))
     turned = dot(high, get(names[0]))
     if fine:
         turned = turned + (dot(low, get(names[0])) + dot(high, get(names[1])))
-    high, low = halves(turned)
+    turned = jnp.concatenate(
+        [turned[at * height : (at + 1) * height] for at in range(count)], axis=1
+    )
+    high = turned.astype(bf16)
     both_parts = dot(get("down"), high)
-    if fine:
-        both_parts = both_parts + (dot(get("down"), low) + dot(get("down_low"), high))
-    upper, lower = both_parts[:height], both_parts[height:]
-    if inverse:
-        return upper[:, :depth] - lower[:, depth:], lower[:, :depth] + upper[:, depth:]
-    return upper[:, :depth] + lower[:, depth:], upper[:, depth:] - lower[:, :depth]
-
-
-def coil_term(real, imag, coil, maps, kspace, mask, get):
-    map_real, map_imag = maps[coil, 0, 0], maps[coil, 1, 0]
-    image = jnp.concatenate(
-        [map_real * real - map_imag * imag, map_real * imag + map_imag * real], axis=1
-    )
-    freq_real, freq_imag = spectrum(image, get, False, False)
-    if kspace is not None:
-        freq_real, freq_imag = freq_real - kspace[coil, 0, 0], freq_imag - kspace[coil, 1, 0]
-    freq = jnp.concatenate([mask * freq_real, mask * freq_imag], axis=1)
-    back_real, back_imag = spectrum(freq, get, True, kspace is not None)
-    return (
-        map_real * back_real + map_imag * back_imag,
-        map_real * back_imag - map_imag * back_real,
-    )
+    results = []
+    for at in range(count):
+        start = 2 * at * depth
+        upper = both_parts[:height, start : start + 2 * depth]
+        lower = both_parts[height:, start : start + 2 * depth]
+        if inverse:
+            results.append(
+                (upper[:, :depth] - lower[:, depth:], lower[:, :depth] + upper[:, depth:])
+            )
+        else:
+            results.append(
+                (upper[:, :depth] + lower[:, depth:], upper[:, depth:] - lower[:, :depth])
+            )
+    return results
 
 
 def normal_part(real, imag, maps, kspace, mask, get):
+    images = []
+    for coil in range(maps.shape[0]):
+        map_real, map_imag = maps[coil, 0, 0], maps[coil, 1, 0]
+        images.append(
+            jnp.concatenate(
+                [map_real * real - map_imag * imag, map_real * imag + map_imag * real], axis=1
+            )
+        )
+    masked = []
+    for coil, (freq_real, freq_imag) in enumerate(spectrum(images, get, False, False)):
+        if kspace is not None:
+            freq_real = freq_real - kspace[coil, 0, 0]
+            freq_imag = freq_imag - kspace[coil, 1, 0]
+        masked.append(jnp.concatenate([mask * freq_real, mask * freq_imag], axis=1))
     total = None
-    for coil in range(maps.shape[0]):
-        term = coil_term(real, imag, coil, maps, kspace, mask, get)
+    for coil, (real, imag) in enumerate(spectrum(masked, get, True, kspace is not None)):
+        map_real, map_imag = maps[coil, 0, 0], maps[coil, 1, 0]
+        term = (map_real * real + map_imag * imag, map_real * imag - map_imag * real)
         total = term if total is None else (total[0] + term[0], total[1] + term[1])
     return total
 
@@ -587,7 +597,6 @@
         (mids, bf16),
         ((hidden, 9 * channels), bf16),
     ]
-    ways = (coils, slabs, coils, slabs, slabs, slabs, slabs, coils, coils, coils, coils)
     changes = pl.pallas_call(
         lambda *refs: step_kernel(places, *refs),
         out_shape=pltpu.VMEM((3, 2, rows, depth), f32),
@@ -597,7 +606,7 @@
         + [pltpu.SemaphoreType.DMA((11,))]
         + [pltpu.VMEM(shape, kind) for shape, kind in buffers]
         + [pltpu.SemaphoreType.DMA((4,))]
-        + [pltpu.SemaphoreType.DMA((size,)) for size in ways for _ in range(2)],
+        + [pltpu.SemaphoreType.DMA] * 22,
         compiler_params=pltpu.CompilerParams(
             collective_id=0, has_side_effects=True, vmem_limit_bytes=40 << 20
         ),

time: 37.9 us -> 36.2 us (0.955)
  Pallas kernels: 36.3 us -> 34.6 us
    pallas_call x1, Pallas kernels: 36.3 us -> 34.6 us  [on_device(): pl.pallas_call(lambda *refs: step_kernel(places, *refs), out_shape=pltpu....]
where the time goes in v3:
time: 36.2 us; the launch traced here: 36.1 us
  Pallas kernels  34.6 us (96%)
  between operations  0.71 us (2%)
  other arithmetic  0.69 us (2%)
    pallas_call x1, Pallas kernels, on_device(): pl.pallas_call(lambda *refs: step_kernel(places, *refs), out_shape=pltpu....  34.6 us

profile of v3, /device:TPU:0, one launch (start us, length us, event | category | flops | bytes accessed | tf_op | source)
XLA Modules:
  0.0 36.1 jit_solution(7539765217210485411)
XLA Ops:
  0.6 0.0 copy-start
  0.6 0.0 copy-start.1
  0.7 0.0 copy-start.2
  0.7 0.0 copy-start.3
  0.7 34.6 %step.1 = f32[3,2,64,128]{3,2,1,0:T(8,128)S(1)} custom-call(f32[2,2,1,256,128]{4,3,2,1,0:T(8,128)} %refs_0_.1, f32[2,2,1,256,128]{4,3,2,1,0:T(8,128)} %refs_1_.1, s32[256,128]{1,0:T(8,128)} %refs_2_.1, f32[2,1,64,128]{3,2,1,0:T(8,128)} %refs_3_.1, s32[2,1,64,128]{3,2,1,0:T(8,128)} %refs_4_.1, f32[2,1,64,128]{3,2,1,0:T(8,128)} %refs_5_.1, ...), custom_call_target="tpu_custom_call" | custom-call | tf_op jit(solution)/shard_map/step/pallas_call | solution.py:600
  35.3 0.0 copy-done
  35.3 0.0 copy-done.1
  35.3 0.0 copy-done.2
  35.4 0.0 copy-done.3
  35.4 0.7 %fusion.1 = (f32[2,1,64,128]{3,2,1,0:T(8,128)}, f32[2,1,64,128]{3,2,1,0:T(8,128)}, f32[2,1,64,128]{3,2,1,0:T(8,128)}) fusion(f32[2,1,64,128]{3,2,1,0:T(8,128)S(1)} %copy-done, f32[2,1,64,128]{3,2,1,0:T(8,128)S(1)} %copy-done.3, f32[3,2,64,128]{3,2,1,0:T(8,128)S(1)} %step.1, s32[2,1,64,128]{3,2,1,0:T(8,128)S(1)} %copy-done.2, f32[2,1,64,128]{3,2,1,0:T(8,128)S(1)} %copy-done.1), kind=kLoop, calls=%fused_computation.2 | loop fusion | flops 114688 | bytes 655360
Async XLA Ops:
  0.6 34.7 %copy-start = (f32[2,1,64,128]{3,2,1,0:T(8,128)S(1)}, f32[2,1,64,128]{3,2,1,0:T(8,128)}, u32[]{:S(2)}) copy-start(f32[2,1,64,128]{3,2,1,0:T(8,128)} %refs_5_.1) | copy-start | bytes 196612
  0.6 34.7 %copy-start.1 = (f32[2,1,64,128]{3,2,1,0:T(8,128)S(1)}, f32[2,1,64,128]{3,2,1,0:T(8,128)}, u32[]{:S(2)}) copy-start(f32[2,1,64,128]{3,2,1,0:T(8,128)} %refs_3_.1) | copy-start | bytes 196612
  0.7 34.7 %copy-start.2 = (s32[2,1,64,128]{3,2,1,0:T(8,128)S(1)}, s32[2,1,64,128]{3,2,1,0:T(8,128)}, u32[]{:S(2)}) copy-start(s32[2,1,64,128]{3,2,1,0:T(8,128)} %refs_4_.1) | copy-start | bytes 196612
  0.7 34.7 %copy-start.3 = (f32[2,1,64,128]{3,2,1,0:T(8,128)S(1)}, f32[2,1,64,128]{3,2,1,0:T(8,128)}, u32[]{:S(2)}) copy-start(f32[2,1,64,128]{3,2,1,0:T(8,128)} %param.16) | copy-start | bytes 196612

commit v4 on v3

--- a/solution.py
+++ b/solution.py
@@ -228,7 +228,8 @@
 
 
 def build_mid(raw, flip, get, target, slices):
-    outs, hidden = raw.shape[3], target.shape[0] * target.shape[1]
+    outs = raw.shape[3]
+    hidden = outs * slices
     out_count, starts, width = groups_of(slices, hidden)
     blocks = []
     for dx in range(3):
@@ -252,8 +253,9 @@
                     at = (dx * 9 + tap) * outs
                     term = jnp.where(keeps[dx], wide[at : at + outs], 0.0)
                     block = term if block is None else block + term
+                at = (tap % 3 * out_count + out_at) * outs
                 target[
-                    index, out_at * outs : (out_at + 1) * outs, tap * width : (tap + 1) * width
+                    index, at : at + outs, tap // 3 * width : (tap // 3 + 1) * width
                 ] = block.astype(bf16)
 
 
@@ -282,18 +284,19 @@
 def conv_mid(values, weights, depth, slices):
     cols = values.shape[1] - 2 * depth
     _, starts, width = groups_of(slices, values.shape[0])
-    turned = [shifted(values, tap, depth).astype(bf16) for tap in range(3)]
+    held = values.astype(bf16)
     totals = []
     for index, start in enumerate(starts):
         stacked = jnp.concatenate(
-            [
-                turned[dz][start : start + width, dy * depth : dy * depth + cols]
-                for dy in range(3)
-                for dz in range(3)
-            ],
+            [held[start : start + width, dy * depth : dy * depth + cols] for dy in range(3)],
             axis=0,
         )
-        totals.append(dot(weights[index], stacked))
+        products = dot(weights[index], stacked)
+        rows = products.shape[0] // 3
+        total = products[rows : 2 * rows]
+        for dz in (0, 2):
+            total = total + shifted(products[dz * rows : (dz + 1) * rows], dz, depth)
+        totals.append(total)
     return jnp.concatenate(totals, axis=0)
 
 
@@ -325,7 +328,8 @@
     (padded, padded_iterate, padded_fields, padded_relaxed, flats, work, rows_work,
      own_iterate, own_fields, all_iterate, halo, parts_send, parts, window_send, windows,
      fields_send, fields, delta_send, delta, grads_send, grads_back, own_pulled, all_pulled,
-     sums_send, sums, first, second, last, first_t, second_t, last_t, halo_sem, *sems) = refs
+     sums_send, sums, first, second, last, first_t, second_t, last_t, exact, halo_sem, back_send,
+     back_recv, pulled_send, pulled_recv, *sems) = refs
     channels = []
     for index, (axis, how, source, target) in enumerate((
         ("coil", "all", own_iterate, all_iterate),
@@ -333,16 +337,12 @@
         ("coil", "row", parts_send, parts),
         ("slab", "row", window_send, windows),
         ("slab", "row", delta_send, delta),
-        ("slab", "row", grads_send.at[0], grads_back.at[0]),
-        ("slab", "row", grads_send.at[1], grads_back.at[1]),
-        ("coil", "all", own_pulled.at[0], all_pulled.at[0]),
-        ("coil", "all", own_pulled.at[1], all_pulled.at[1]),
         ("coil", "row", sums_send.at[0], sums.at[0]),
         ("coil", "row", sums_send.at[1], sums.at[1]),
     )):
         channels.append(Channel(axis, how, source, target, sems[2 * index], sems[2 * index + 1]))
     (iterate_way, field_way, part_way, window_way, delta_way, *later) = channels
-    grad_ways, pulled_ways, sum_ways = later[:2], later[2:4], later[4:]
+    sum_ways = later
 
     height, depth = mask.shape
     coils, _, rows, _ = all_iterate.shape
@@ -477,6 +477,51 @@
         window_send[piece] = padded_relaxed[:, piece * own : piece * own + window].astype(bf16)
     window_way.start()
     windows[my_slab] = window_send[my_slab]
+    pair = 2 if slices % 2 == 0 else 1
+    groups = slices // pair
+    my_group = lax.div(my_slab, pair)
+
+    def send_back(field):
+        for step in range(1, slices):
+            rank = lax.rem(my_slab + step, slices)
+            group = lax.rem(my_group + groups - lax.div(rank, pair), groups)
+            pltpu.make_async_remote_copy(
+                src_ref=grads_send.at[field, rank],
+                dst_ref=grads_back.at[field, my_slab],
+                send_sem=back_send.at[field],
+                recv_sem=back_recv.at[field, group],
+                device_id=place_of("slab", rank),
+                device_id_type=MESH,
+            ).start()
+
+    def pass_on(field):
+        for step in range(groups):
+            count = pair if step else pair - 1
+            group = lax.rem(my_group + step, groups)
+            if count:
+                landed = grads_back.at[field, 0:count]
+                pltpu.make_async_copy(landed, landed, back_recv.at[field, step]).wait()
+            for index in range(pair):
+                piece = group * pair + index
+                own_pulled[field, piece] = (
+                    exact[field, piece] + grads_back[field, piece].astype(f32)
+                ).astype(bf16)
+            span = pl.ds(group * pair, pair)
+            for turn in range(1, coils):
+                pltpu.make_async_remote_copy(
+                    src_ref=own_pulled.at[field, span],
+                    dst_ref=all_pulled.at[field, my_coil, span],
+                    send_sem=pulled_send.at[field],
+                    recv_sem=pulled_recv.at[field],
+                    device_id=place_of("coil", lax.rem(my_coil + turn, coils)),
+                    device_id_type=MESH,
+                ).start()
+        all_pulled[field, my_coil] = own_pulled[field]
+
+    for piece in range(slices):
+        at = slice(piece * own, (piece + 1) * own)
+        exact[0, piece] = (2 * bits[:, 0, at] - 1).astype(f32)
+        exact[1, piece] = adjoint[:, 0, at]
     fields[my_slab] = fields_send[my_slab]
     field_way.finish()
     grads = []
@@ -497,30 +542,32 @@
     for field in range(2):
         grad1 = conv_mid(grads[field] * slope2, second_t, depth, slices) * slope1
         grads_send[field] = store(conv_out(grad1, first_t, depth))
-        grad_ways[field].start()
+        send_back(field)
         grads_back[field, my_slab] = grads_send[field, my_slab]
     act2 = inside(cut(act2, 1, 1), 3)
     delta_out = store(conv_out(act2, last, depth))
 
-    exact = ((2 * bits[:, 0] - 1).astype(f32), adjoint[:, 0])
-    backs = []
     for field in range(2):
-        grad_ways[field].finish()
-        back = jnp.concatenate(
-            [grads_back[field, piece].astype(f32) for piece in range(slices)], axis=1
-        )
-        backs.append(back)
-        own_pulled[field] = (exact[field] + back).astype(bf16)
-        pulled_ways[field].start()
-        all_pulled[field, my_coil] = own_pulled[field]
+        pass_on(field)
         if field == 0:
             delta_send[...] = delta_out
             delta_way.start()
             delta[my_slab] = delta_send[my_slab]
     partial = []
     for field in range(2):
-        pulled_ways[field].finish()
-        real, imag = column(all_pulled.at[field], 0), column(all_pulled.at[field], 1)
+        landed = all_pulled.at[field, 0 : coils - 1]
+        for sem in (pulled_send, pulled_recv):
+            pltpu.make_async_copy(landed, landed, sem.at[field]).wait()
+        real, imag = (
+            jnp.concatenate(
+                [
+                    all_pulled[field, piece // slices, piece % slices, part].astype(f32)
+                    for piece in range(coils * slices)
+                ],
+                axis=0,
+            )
+            for part in range(2)
+        )
         total = normal_part(real, imag, maps, None, weight, get)
         for part in range(2):
             padded[part, 0:height] = total[part]
@@ -531,6 +578,15 @@
         sum_ways[field].start()
         partial.append(padded[:, pl.ds(coil_base, rows)])
 
+    backs = []
+    for field in range(2):
+        landed = grads_back.at[field, 0 : slices - 1]
+        pltpu.make_async_copy(landed, landed, back_send.at[field]).wait()
+        backs.append(
+            jnp.concatenate(
+                [grads_back[field, piece].astype(f32) for piece in range(slices)], axis=1
+            )
+        )
     delta_way.finish()
     for piece in range(slices):
         at = piece * own
@@ -563,7 +619,7 @@
     operands = (coil_maps, kspace, sample_mask, iterate, probe_bits, adjoint, *raws,
                 jnp.asarray(table))
     _, starts, width = groups_of(slabs, hidden)
-    mids = (len(starts), hidden // len(starts), 9 * width)
+    mids = (len(starts), 3 * hidden // len(starts), 3 * width)
     buffers = [
         ((2, height + 2 * reach + 8, depth), f32),
         ((2, height + 2 * reach + 8, depth), f32),
@@ -586,8 +642,8 @@
         ((slabs, 2, own, depth), bf16),
         ((2, slabs, 2, own, depth), bf16),
         ((2, slabs, 2, own, depth), bf16),
-        ((2, 2, rows, depth), bf16),
-        ((2, coils, 2, rows, depth), bf16),
+        ((2, slabs, 2, own, depth), bf16),
+        ((2, coils, slabs, 2, own, depth), bf16),
         ((2, coils, 2, rows, depth), bf16),
         ((2, coils, 2, rows, depth), bf16),
         ((hidden, 9 * channels), bf16),
@@ -596,7 +652,9 @@
         ((9 * channels, hidden), bf16),
         (mids, bf16),
         ((hidden, 9 * channels), bf16),
+        ((2, slabs, 2, own, depth), f32),
     ]
+    groups = slabs // 2 if slabs % 2 == 0 else slabs
     changes = pl.pallas_call(
         lambda *refs: step_kernel(places, *refs),
         out_shape=pltpu.VMEM((3, 2, rows, depth), f32),
@@ -606,7 +664,9 @@
         + [pltpu.SemaphoreType.DMA((11,))]
         + [pltpu.VMEM(shape, kind) for shape, kind in buffers]
         + [pltpu.SemaphoreType.DMA((4,))]
-        + [pltpu.SemaphoreType.DMA] * 22,
+        + [pltpu.SemaphoreType.DMA((2,)), pltpu.SemaphoreType.DMA((2, groups))]
+        + [pltpu.SemaphoreType.DMA((2,))] * 2
+        + [pltpu.SemaphoreType.DMA] * 14,
         compiler_params=pltpu.CompilerParams(
             collective_id=0, has_side_effects=True, vmem_limit_bytes=40 << 20
         ),

time: 36.2 us -> 35.6 us (0.983)
  Pallas kernels: 34.6 us -> 34 us
    pallas_call x1, Pallas kernels: 34.6 us -> 34 us  [on_device(): pl.pallas_call(lambda *refs: step_kernel(places, *refs), out_shape=pltpu....]
where the time goes in v4:
time: 35.6 us; the launch traced here: 35.4 us
  Pallas kernels  34 us (96%)
  between operations  0.71 us (2%)
  other arithmetic  0.69 us (2%)
    pallas_call x1, Pallas kernels, on_device(): pl.pallas_call(lambda *refs: step_kernel(places, *refs), out_shape=pltpu....  34 us

profile of v4, /device:TPU:0, one launch (start us, length us, event | category | flops | bytes accessed | tf_op | source)
XLA Modules:
  0.0 35.4 jit_solution(5705912466226588229)
XLA Ops:
  0.6 0.0 copy-start
  0.6 0.0 copy-start.1
  0.7 0.0 copy-start.2
  0.7 0.0 copy-start.3
  0.7 34.0 %step.1 = f32[3,2,64,128]{3,2,1,0:T(8,128)S(1)} custom-call(f32[2,2,1,256,128]{4,3,2,1,0:T(8,128)} %refs_0_.1, f32[2,2,1,256,128]{4,3,2,1,0:T(8,128)} %refs_1_.1, s32[256,128]{1,0:T(8,128)} %refs_2_.1, f32[2,1,64,128]{3,2,1,0:T(8,128)} %refs_3_.1, s32[2,1,64,128]{3,2,1,0:T(8,128)} %refs_4_.1, f32[2,1,64,128]{3,2,1,0:T(8,128)} %refs_5_.1, ...), custom_call_target="tpu_custom_call" | custom-call | tf_op jit(solution)/shard_map/step/pallas_call | solution.py:658
  34.7 0.0 copy-done
  34.7 0.0 copy-done.1
  34.7 0.0 copy-done.2
  34.7 0.0 copy-done.3
  34.7 0.7 %fusion.1 = (f32[2,1,64,128]{3,2,1,0:T(8,128)}, f32[2,1,64,128]{3,2,1,0:T(8,128)}, f32[2,1,64,128]{3,2,1,0:T(8,128)}) fusion(f32[2,1,64,128]{3,2,1,0:T(8,128)S(1)} %copy-done, f32[2,1,64,128]{3,2,1,0:T(8,128)S(1)} %copy-done.3, f32[3,2,64,128]{3,2,1,0:T(8,128)S(1)} %step.1, s32[2,1,64,128]{3,2,1,0:T(8,128)S(1)} %copy-done.2, f32[2,1,64,128]{3,2,1,0:T(8,128)S(1)} %copy-done.1), kind=kLoop, calls=%fused_computation.2 | loop fusion | flops 114688 | bytes 655360
Async XLA Ops:
  0.6 34.0 %copy-start = (f32[2,1,64,128]{3,2,1,0:T(8,128)S(1)}, f32[2,1,64,128]{3,2,1,0:T(8,128)}, u32[]{:S(2)}) copy-start(f32[2,1,64,128]{3,2,1,0:T(8,128)} %refs_5_.1) | copy-start | bytes 196612
  0.6 34.0 %copy-start.1 = (f32[2,1,64,128]{3,2,1,0:T(8,128)S(1)}, f32[2,1,64,128]{3,2,1,0:T(8,128)}, u32[]{:S(2)}) copy-start(f32[2,1,64,128]{3,2,1,0:T(8,128)} %refs_3_.1) | copy-start | bytes 196612
  0.7 34.0 %copy-start.2 = (s32[2,1,64,128]{3,2,1,0:T(8,128)S(1)}, s32[2,1,64,128]{3,2,1,0:T(8,128)}, u32[]{:S(2)}) copy-start(s32[2,1,64,128]{3,2,1,0:T(8,128)} %refs_4_.1) | copy-start | bytes 196612
  0.7 34.0 %copy-start.3 = (f32[2,1,64,128]{3,2,1,0:T(8,128)S(1)}, f32[2,1,64,128]{3,2,1,0:T(8,128)}, u32[]{:S(2)}) copy-start(f32[2,1,64,128]{3,2,1,0:T(8,128)} %param.16) | copy-start | bytes 196612

commit v5 on v4

--- a/solution.py
+++ b/solution.py
@@ -35,7 +35,7 @@
         )
 
     def start(self):
-        for step in range(1, self.size):
+        for step in far_first(self.size):
             rank = lax.rem(self.mine + step, self.size)
             self.copy(rank, self.mine, rank).start()
 
@@ -43,6 +43,10 @@
         landed = self.target.at[0 : self.size - 1]
         for sem in (self.send_sem, self.recv_sem):
             pltpu.make_async_copy(landed, landed, sem).wait()
+
+
+def far_first(size):
+    return sorted(range(1, size), key=lambda step: abs(2 * step - size))
 
 
 def place_of(axis, rank):
@@ -155,7 +159,7 @@
     high, low = halves(jnp.concatenate(images, axis=0))
     turned = dot(high, get(names[0]))
     if fine:
-        turned = turned + (dot(low, get(names[0])) + dot(high, get(names[1])))
+        turned = turned + dot(high, get(names[1]))
     turned = jnp.concatenate(
         [turned[at * height : (at + 1) * height] for at in range(count)], axis=1
     )
@@ -482,7 +486,7 @@
     my_group = lax.div(my_slab, pair)
 
     def send_back(field):
-        for step in range(1, slices):
+        for step in far_first(slices):
             rank = lax.rem(my_slab + step, slices)
             group = lax.rem(my_group + groups - lax.div(rank, pair), groups)
             pltpu.make_async_remote_copy(

time: 35.6 us -> 35.4 us (level)
  no operation moved by 1% of the time
where the time goes in v5:
time: 35.4 us; the launch traced here: 35.2 us
  Pallas kernels  33.8 us (95%)
  between operations  0.71 us (2%)
  other arithmetic  0.69 us (2%)
    pallas_call x1, Pallas kernels, on_device(): pl.pallas_call(lambda *refs: step_kernel(places, *refs), out_shape=pltpu....  33.8 us

profile of v5, /device:TPU:0, one launch (start us, length us, event | category | flops | bytes accessed | tf_op | source)
XLA Modules:
  0.0 35.2 jit_solution(4401251363415866774)
XLA Ops:
  0.6 0.0 copy-start
  0.6 0.0 copy-start.1
  0.7 0.0 copy-start.2
  0.7 0.0 copy-start.3
  0.7 33.8 %step.1 = f32[3,2,64,128]{3,2,1,0:T(8,128)S(1)} custom-call(f32[2,2,1,256,128]{4,3,2,1,0:T(8,128)} %refs_0_.1, f32[2,2,1,256,128]{4,3,2,1,0:T(8,128)} %refs_1_.1, s32[256,128]{1,0:T(8,128)} %refs_2_.1, f32[2,1,64,128]{3,2,1,0:T(8,128)} %refs_3_.1, s32[2,1,64,128]{3,2,1,0:T(8,128)} %refs_4_.1, f32[2,1,64,128]{3,2,1,0:T(8,128)} %refs_5_.1, ...), custom_call_target="tpu_custom_call" | custom-call | tf_op jit(solution)/shard_map/step/pallas_call | solution.py:662
  34.5 0.0 copy-done
  34.5 0.0 copy-done.1
  34.5 0.0 copy-done.2
  34.5 0.0 copy-done.3
  34.5 0.7 %fusion.1 = (f32[2,1,64,128]{3,2,1,0:T(8,128)}, f32[2,1,64,128]{3,2,1,0:T(8,128)}, f32[2,1,64,128]{3,2,1,0:T(8,128)}) fusion(f32[2,1,64,128]{3,2,1,0:T(8,128)S(1)} %copy-done, f32[2,1,64,128]{3,2,1,0:T(8,128)S(1)} %copy-done.3, f32[3,2,64,128]{3,2,1,0:T(8,128)S(1)} %step.1, s32[2,1,64,128]{3,2,1,0:T(8,128)S(1)} %copy-done.2, f32[2,1,64,128]{3,2,1,0:T(8,128)S(1)} %copy-done.1), kind=kLoop, calls=%fused_computation.2 | loop fusion | flops 114688 | bytes 655360
Async XLA Ops:
  0.6 33.9 %copy-start = (f32[2,1,64,128]{3,2,1,0:T(8,128)S(1)}, f32[2,1,64,128]{3,2,1,0:T(8,128)}, u32[]{:S(2)}) copy-start(f32[2,1,64,128]{3,2,1,0:T(8,128)} %refs_5_.1) | copy-start | bytes 196612
  0.6 33.9 %copy-start.1 = (f32[2,1,64,128]{3,2,1,0:T(8,128)S(1)}, f32[2,1,64,128]{3,2,1,0:T(8,128)}, u32[]{:S(2)}) copy-start(f32[2,1,64,128]{3,2,1,0:T(8,128)} %refs_3_.1) | copy-start | bytes 196612
  0.7 33.9 %copy-start.2 = (s32[2,1,64,128]{3,2,1,0:T(8,128)S(1)}, s32[2,1,64,128]{3,2,1,0:T(8,128)}, u32[]{:S(2)}) copy-start(s32[2,1,64,128]{3,2,1,0:T(8,128)} %refs_4_.1) | copy-start | bytes 196612
  0.7 33.9 %copy-start.3 = (f32[2,1,64,128]{3,2,1,0:T(8,128)S(1)}, f32[2,1,64,128]{3,2,1,0:T(8,128)}, u32[]{:S(2)}) copy-start(f32[2,1,64,128]{3,2,1,0:T(8,128)} %param.16) | copy-start | bytes 196612

commit v6 on v4

--- a/solution.py
+++ b/solution.py
@@ -198,6 +198,26 @@
         term = (map_real * real + map_imag * imag, map_real * imag - map_imag * real)
         total = term if total is None else (total[0] + term[0], total[1] + term[1])
     return total
+
+
+def field_turned(real, imag, maps, mask, get):
+    images = []
+    for coil in range(maps.shape[0]):
+        map_real, map_imag = maps[coil, 0, 0], maps[coil, 1, 0]
+        images.append(
+            jnp.concatenate(
+                [map_real * real - map_imag * imag, map_real * imag + map_imag * real], axis=1
+            )
+        )
+    masked = [
+        jnp.concatenate([mask * freq_real, mask * freq_imag], axis=1).astype(bf16)
+        for freq_real, freq_imag in spectrum(images, get, False, False)
+    ]
+    height = real.shape[0]
+    turned = dot(jnp.concatenate(masked, axis=0), get("back")).astype(bf16)
+    return jnp.concatenate(
+        [turned[at * height : (at + 1) * height] for at in range(len(masked))], axis=1
+    )
 
 
 def build_in(flat, flip, get, target, slices):
@@ -568,15 +588,36 @@
             )
             for part in range(2)
         )
-        total = normal_part(real, imag, maps, None, weight, get)
-        for part in range(2):
-            padded[part, 0:height] = total[part]
-            for piece in range(coils):
-                sums_send[field, piece, part] = total[part][
-                    piece * rows : (piece + 1) * rows
-                ].astype(bf16)
-        sum_ways[field].start()
-        partial.append(padded[:, pl.ds(coil_base, rows)])
+        turned = field_turned(real, imag, maps, weight, get)
+        down_at = places["down"][0]
+        for step in (*range(1, coils), 0):
+            rank = lax.rem(my_coil + step, coils)
+            base = pl.multiple_of(rank * rows, 8)
+            left = jnp.concatenate(
+                [
+                    table[pl.ds(pl.multiple_of(down_at + part * height + base, 8), rows), 0:height]
+                    for part in range(2)
+                ],
+                axis=0,
+            )
+            products = dot(left, turned)
+            total = None
+            for coil in range(maps.shape[0]):
+                start = 2 * coil * depth
+                upper = products[:rows, start : start + 2 * depth]
+                lower = products[rows:, start : start + 2 * depth]
+                real = upper[:, :depth] - lower[:, depth:]
+                imag = lower[:, :depth] + upper[:, depth:]
+                map_real = maps[coil, 0, 0, pl.ds(base, rows)]
+                map_imag = maps[coil, 1, 0, pl.ds(base, rows)]
+                term = (map_real * real + map_imag * imag, map_real * imag - map_imag * real)
+                total = term if total is None else (total[0] + term[0], total[1] + term[1])
+            if step:
+                for part in range(2):
+                    sums_send[field, rank, part] = total[part].astype(bf16)
+                sum_ways[field].copy(rank, my_coil, rank).start()
+            else:
+                partial.append(jnp.stack(total))
 
     backs = []
     for field in range(2):

time: 35.6 us -> 35.6 us (level)
  no operation moved by 1% of the time
where the time goes in v6:
time: 35.6 us; the launch traced here: 35.4 us
  Pallas kernels  34 us (96%)
  between operations  0.71 us (2%)
  other arithmetic  0.69 us (2%)
    pallas_call x1, Pallas kernels, on_device(): pl.pallas_call(lambda *refs: step_kernel(places, *refs), out_shape=pltpu....  34 us

profile of v6, /device:TPU:0, one launch (start us, length us, event | category | flops | bytes accessed | tf_op | source)
XLA Modules:
  0.0 35.4 jit_solution(11762320730793894809)
XLA Ops:
  0.6 0.0 copy-start
  0.6 0.0 copy-start.1
  0.7 0.0 copy-start.2
  0.7 0.0 copy-start.3
  0.7 34.0 %step.1 = f32[3,2,64,128]{3,2,1,0:T(8,128)S(1)} custom-call(f32[2,2,1,256,128]{4,3,2,1,0:T(8,128)} %refs_0_.1, f32[2,2,1,256,128]{4,3,2,1,0:T(8,128)} %refs_1_.1, s32[256,128]{1,0:T(8,128)} %refs_2_.1, f32[2,1,64,128]{3,2,1,0:T(8,128)} %refs_3_.1, s32[2,1,64,128]{3,2,1,0:T(8,128)} %refs_4_.1, f32[2,1,64,128]{3,2,1,0:T(8,128)} %refs_5_.1, ...), custom_call_target="tpu_custom_call" | custom-call | tf_op jit(solution)/shard_map/step/pallas_call | solution.py:699
  34.7 0.0 copy-done
  34.7 0.0 copy-done.1
  34.7 0.0 copy-done.2
  34.7 0.0 copy-done.3
  34.7 0.7 %fusion.1 = (f32[2,1,64,128]{3,2,1,0:T(8,128)}, f32[2,1,64,128]{3,2,1,0:T(8,128)}, f32[2,1,64,128]{3,2,1,0:T(8,128)}) fusion(f32[2,1,64,128]{3,2,1,0:T(8,128)S(1)} %copy-done, f32[2,1,64,128]{3,2,1,0:T(8,128)S(1)} %copy-done.3, f32[3,2,64,128]{3,2,1,0:T(8,128)S(1)} %step.1, s32[2,1,64,128]{3,2,1,0:T(8,128)S(1)} %copy-done.2, f32[2,1,64,128]{3,2,1,0:T(8,128)S(1)} %copy-done.1), kind=kLoop, calls=%fused_computation.2 | loop fusion | flops 114688 | bytes 655360
Async XLA Ops:
  0.6 34.1 %copy-start = (f32[2,1,64,128]{3,2,1,0:T(8,128)S(1)}, f32[2,1,64,128]{3,2,1,0:T(8,128)}, u32[]{:S(2)}) copy-start(f32[2,1,64,128]{3,2,1,0:T(8,128)} %refs_5_.1) | copy-start | bytes 196612
  0.6 34.1 %copy-start.1 = (f32[2,1,64,128]{3,2,1,0:T(8,128)S(1)}, f32[2,1,64,128]{3,2,1,0:T(8,128)}, u32[]{:S(2)}) copy-start(f32[2,1,64,128]{3,2,1,0:T(8,128)} %refs_3_.1) | copy-start | bytes 196612
  0.7 34.1 %copy-start.2 = (s32[2,1,64,128]{3,2,1,0:T(8,128)S(1)}, s32[2,1,64,128]{3,2,1,0:T(8,128)}, u32[]{:S(2)}) copy-start(s32[2,1,64,128]{3,2,1,0:T(8,128)} %refs_4_.1) | copy-start | bytes 196612
  0.7 34.1 %copy-start.3 = (f32[2,1,64,128]{3,2,1,0:T(8,128)S(1)}, f32[2,1,64,128]{3,2,1,0:T(8,128)}, u32[]{:S(2)}) copy-start(f32[2,1,64,128]{3,2,1,0:T(8,128)} %param.16) | copy-start | bytes 196612
